TPU v7x, 32 devices: a whole 2x2x4 slice. The times are simulated.
32 devices in a mesh: gx: 4 (over x, core), gy: 8 (over z, y).
Axes of the slice: x: 2, y: 2, z: 4, core: 2. Of those that a mesh axis runs over, the one named last changes fastest.
Arguments:
- state_field: float32 [128, 128, 16, 256], P('gx', 'gy'), may hold values from -80 to 80
- start_basis: float32 [256, 32], replicated, may hold values from -6 to 6
Outputs:
- core_tensor: float32 [128, 128, 512], P('gx', 'gy')
- z_factor: float32 [256, 32], replicated
- x_triangle: float32 [128, 128], replicated
All inputs are finite; a program needn't handle non-finite values.
Results may differ from a plain program's by a relative error of at most 0.0003.
Values sent between devices are 32-bit elements; how exact they have to be, the bound alone decides.
No kernel may reach another device: no remote copies, remote signals or barrier semaphores. Data moves between devices by JAX's collectives and lax.ppermute only.
A program may use at most 64 MiB of HBM per device.

v0:
```python
import functools

import jax
import jax.numpy as jnp
from jax import lax
from jax.experimental import pallas as pl
from jax.experimental.pallas import tpu as pltpu
from jax.sharding import PartitionSpec as P


ITERS = 3
F32, BF16 = jnp.float32, jnp.bfloat16
LANES, SUBLANES = 128, 8

precise = lax.Precision.HIGHEST
ROWS_BY_ROWS = (((1,), (1,)), ((), ()))
COLUMNS_BY_COLUMNS = (((0,), (0,)), ((), ()))
VMEM = pl.BlockSpec(memory_space=pltpu.VMEM)
SMEM = pl.BlockSpec(memory_space=pltpu.SMEM)
HBM = pl.BlockSpec(memory_space=pltpu.HBM)
SMALL = pltpu.CompilerParams(vmem_limit_bytes=32 << 20)


def bits(size):
    return [1 << b for b in range(size.bit_length() - 1)]


def partner(value, x_mask, y_mask=0):
    x_size, y_size = lax.axis_size("gx"), lax.axis_size("gy")
    pairs = [
        (x * y_size + y, (x ^ x_mask) * y_size + (y ^ y_mask)) for x in range(x_size) for y in range(y_size)
    ]
    return lax.ppermute(value, ("gx", "gy"), pairs)


def summed(value):
    masks = [(bit, 0) for bit in bits(lax.axis_size("gx"))[1:]] + [(0, bit) for bit in bits(lax.axis_size("gy"))]
    while masks:
        first, masks = masks[0], masks[1:]
        near = value + partner(value, *first)
        if masks:
            second, masks = masks[0], masks[1:]
            both = (first[0] ^ second[0], first[1] ^ second[1])
            near = near + (partner(value, *second) + partner(value, *both))
        value = near
    return value


def in_two(value):
    high = value.astype(BF16)
    return high, (value - high.astype(F32)).astype(BF16)


def tiles(value):
    rows, columns = value.shape
    return [
        [value[r : r + SUBLANES, c : min(c + LANES, columns)] for c in range(0, columns, LANES)]
        for r in range(0, rows, SUBLANES)
    ]


def joined(groups):
    return jnp.concatenate([jnp.concatenate(group, axis=1) for group in groups], axis=0)


def eliminated(gram, extra):
    gram = [list(group) for group in gram]
    extra = [list(group) for group in extra]
    row_id = lax.broadcasted_iota(jnp.int32, (SUBLANES, LANES), 0)

    def row(tile, r):
        return jnp.broadcast_to(tile[r : r + 1, :], tile.shape)

    def column(tile, c):
        return jnp.broadcast_to(tile[:, c : c + 1], (SUBLANES, LANES))

    def spread(tile, r):
        return jnp.take_along_axis(tile, jnp.full(tile.shape, r, jnp.int32), axis=0)

    def less(tile, factor, other):
        return tile - factor[:, : tile.shape[1]] * other

    for g in range(len(gram)):
        at, first = divmod(g * SUBLANES, LANES)
        both = [gram[h] + extra[h] for h in range(len(gram))]
        rows = [[row(t, q) for t in both[g]] for q in range(SUBLANES)]
        pivots = [column(gram[g][at], first + b) for b in range(SUBLANES)]
        block = [[spread(pivots[b], a) if b >= a else None for b in range(SUBLANES)] for a in range(SUBLANES)]
        below = range(g + 1, len(gram))
        columns = {h: [column(gram[h][at], first + q) for q in range(SUBLANES)] for h in below}
        scales, inverses = [], []
        for q in range(SUBLANES):
            scales.append(lax.rsqrt(block[q][q]))
            inverses.append(scales[q] * scales[q])
            for b in range(q + 1, SUBLANES):
                factor = block[q][b] * inverses[q]
                for c in range(b, SUBLANES):
                    block[b][c] = block[b][c] - factor * block[q][c]
                rows[b] = [less(t, factor, r) for t, r in zip(rows[b], rows[q])]
                for h in below:
                    columns[h][b] = columns[h][b] - factor * columns[h][q]
        for h in below:
            for q in range(SUBLANES):
                factor = columns[h][q] * inverses[q]
                both[h] = [less(t, factor, r) for t, r in zip(both[h], rows[q])]
        for q in range(SUBLANES):
            both[g] = [
                jnp.where((row_id == q)[:, : t.shape[1]], r * scales[q][:, : t.shape[1]], t)
                for t, r in zip(both[g], rows[q])
            ]
        for h in range(g, len(gram)):
            gram[h], extra[h] = both[h][: len(gram[h])], both[h][len(gram[h]) :]
    return gram, extra


def orth_pass(rows, *more):
    inner_gram = lax.dot_general(rows, rows, ROWS_BY_ROWS, precision=precise, preferred_element_type=F32)
    widths = [v.shape[1] for v in (rows, *more)]
    extra = [sum(parts, []) for parts in zip(*(tiles(v) for v in (rows, *more)))]
    groups = eliminated(tiles(inner_gram), extra)[1]
    out, at = [], 0
    for width in widths:
        count = -(-width // LANES)
        out.append(joined([group[at : at + count] for group in groups]))
        at += count
    return out


def triangle_ids(n):
    return lax.broadcasted_iota(jnp.int32, (n, n), 0), lax.broadcasted_iota(jnp.int32, (n, n), 1)


def folded(full):
    half = full.shape[0] // 2
    r, c = triangle_ids(half)
    corner = full[half:, half:]
    diagonal = jnp.sum(jnp.where(r == c, corner, 0.0), axis=0, keepdims=True)
    return jnp.where(r > c, corner, full[:half, :half]), full[:half, half:], diagonal


def opened(fold, upper, diagonal):
    half = fold.shape[0]
    r, c = triangle_ids(half)
    turned = fold.T
    first = jnp.where(c >= r, fold, turned)
    second = jnp.where(r > c, fold, jnp.where(r == c, jnp.broadcast_to(diagonal, fold.shape), turned))
    return jnp.concatenate(
        [jnp.concatenate([first, upper], axis=1), jnp.concatenate([upper.T, second], axis=1)], axis=0
    )


def species_weights(rows, repeat):
    high, low = in_two(jnp.concatenate([rows] * repeat, axis=0).T)
    weights = jnp.concatenate([high, low], axis=1)
    return jnp.concatenate([weights, weights], axis=0)


def times(value, weights):
    out = jnp.dot(jnp.concatenate(in_two(value), axis=1), weights, preferred_element_type=F32)
    half = out.shape[1] // 2
    return out[:, :half] + out[:, half:]


def packed(narrow, first, count, stride, rank):
    lane = lax.broadcasted_iota(jnp.int32, (count, LANES), 1)
    pack = LANES // rank
    out = narrow[pl.ds(first + pack - 1, count, stride=stride), :]
    for q in range(pack - 2, -1, -1):
        out = jnp.where(lane < (q + 1) * rank, narrow[pl.ds(first + q, count, stride=stride), :], out)
    return out


def gram_kernel(cuts, place, field, mine, other, held, arrived):
    copies = [
        pltpu.make_async_copy(field.at[a:b], held.at[a:b], arrived.at[i])
        for i, (a, b) in enumerate(zip(cuts[:-1], cuts[1:]))
    ]
    for copy in copies:
        copy.start()
    square = cross = 0.0
    for copy, a, b in zip(copies, cuts[:-1], cuts[1:]):
        copy.wait()
        high, low = in_two(held[a:b])
        square = square + lax.dot_general(high, high, COLUMNS_BY_COLUMNS, preferred_element_type=F32)
        cross = cross + lax.dot_general(high, low, COLUMNS_BY_COLUMNS, preferred_element_type=F32)
    fold, upper, diagonal = folded(square + (cross + cross.T))
    half = fold.shape[0]
    edge = SUBLANES
    even = place[0] & 1 == 0

    def put(first, second):
        first[:half] = fold
        first[half:] = upper[:edge]
        second[: half - edge] = upper[edge:]
        second[half - edge :] = jnp.broadcast_to(diagonal, (2 * edge, half))

    @pl.when(even)
    def _():
        put(mine, other)

    @pl.when(jnp.logical_not(even))
    def _():
        put(other, mine)


def local_gram(place, unfolded):
    rows, z = unfolded.shape
    cuts = [0, rows // 8, rows // 2, rows]
    out = jax.ShapeDtypeStruct((z // 2 + SUBLANES, z // 2), F32)
    return pl.pallas_call(
        functools.partial(gram_kernel, cuts),
        out_shape=[out, out, jax.ShapeDtypeStruct((rows, z), F32)],
        in_specs=[SMEM, HBM],
        out_specs=[VMEM] * 3,
        scratch_shapes=[pltpu.SemaphoreType.DMA((len(cuts) - 1,))],
        compiler_params=pltpu.CompilerParams(vmem_limit_bytes=32 << 20),
        name="gram",
    )(place, unfolded)


def begin_kernel(place, mine, other, start, basis, image, gram):
    half = mine.shape[1]
    edge = SUBLANES
    even = place[0] & 1 == 0
    first = jnp.where(even, mine[...], other[...])
    second = jnp.where(even, other[...], mine[...])
    gram[...] = opened(
        first[:half],
        jnp.concatenate([first[half:], second[: half - edge]], axis=0),
        second[half - edge : half - edge + 1],
    )
    basis[...] = start[...]

    def multiplied():
        return jnp.dot(basis[...], gram[...], precision=precise, preferred_element_type=F32)

    @pl.loop(0, ITERS - 2)
    def _(iteration):
        basis[...] = orth_pass(*orth_pass(multiplied()))[0]

    basis[...] = orth_pass(multiplied())[0]
    image[...] = multiplied()


def begin(place, mine, other, start_rows):
    z = start_rows.shape[1]
    rows = jax.ShapeDtypeStruct(start_rows.shape, F32)
    return pl.pallas_call(
        begin_kernel,
        out_shape=[rows, rows, jax.ShapeDtypeStruct((z, z), F32)],
        in_specs=[SMEM] + [VMEM] * 3,
        out_specs=[VMEM] * 3,
        compiler_params=SMALL,
        name="begin",
    )(place, mine, other, start_rows)


def finish_kernel(basis, gram, out, again, factor):
    rank = basis.shape[0]
    r, c = triangle_ids(rank)
    rows, turn = orth_pass(basis[...], jnp.where(r == c, 1.0, 0.0))
    rows = jnp.dot(rows, gram[...], precision=precise, preferred_element_type=F32)
    for _ in range(2):
        rows, turn = orth_pass(rows, turn)
    out[...] = rows
    again[...] = rows
    factor[...] = turn


def finish(basis, gram):
    rank, z = basis.shape
    return pl.pallas_call(
        finish_kernel,
        out_shape=[jax.ShapeDtypeStruct((rank, z), F32)] * 2 + [jax.ShapeDtypeStruct((rank, rank), F32)],
        in_specs=[VMEM] * 2,
        out_specs=[VMEM] * 3,
        compiler_params=SMALL,
        cost_estimate=pl.CostEstimate(flops=1 << 30, bytes_accessed=1 << 24, transcendentals=0),
        name="finish",
    )(basis, gram)


def ahead_kernel(d, share, skip, species, place, field, image, out, narrow):
    count, x_cells, width = out.shape
    rank = image.shape[0]
    across = count * species
    start = pl.multiple_of(((place[0] ^ d) * share + skip) * species, species)
    cells = field[:, pl.ds(start, across), :]
    narrow[...] = times(cells.reshape(x_cells * across, cells.shape[2]), species_weights(image[...], LANES // rank))
    for y in range(count):
        for t in range(width // LANES):
            out[y, :, t * LANES : (t + 1) * LANES] = packed(
                narrow, y * species + t * (LANES // rank), x_cells, across, rank
            )


def contract_ahead(place, field, image, x_cells, y_cells, species, share, d, skip, count):
    z = field.shape[1]
    rank = image.shape[0]
    return pl.pallas_call(
        functools.partial(ahead_kernel, d, share, skip, species),
        out_shape=jax.ShapeDtypeStruct((count, x_cells, species * rank), F32),
        in_specs=[SMEM, VMEM, VMEM],
        out_specs=VMEM,
        scratch_shapes=[pltpu.VMEM((x_cells * count * species, LANES), F32)],
        compiler_params=SMALL,
        cost_estimate=pl.CostEstimate(flops=1 << 30, bytes_accessed=1 << 22, transcendentals=0),
    )(place, field.reshape(x_cells, y_cells * species, z), image)


def core_kernel(species, y_cells, place, field, basis, core, *refs):
    outs, (weights, narrow, strip) = refs[:-3], refs[-3:]
    share, step, width = outs[0].shape
    rank = basis.shape[0]
    cells = core.shape[0]
    half = len(outs)
    near = place[0] // half * half

    @pl.when(pl.program_id(0) == 0)
    def _():
        weights[...] = species_weights(basis[...], LANES // rank)

    block = narrow.shape[0]
    narrow[...] = times(field[pl.ds(pl.multiple_of(pl.program_id(0) * block, block), block), :], weights[...])
    for t in range(width // LANES):
        lanes = slice(t * LANES, (t + 1) * LANES)
        strip[...] = packed(narrow, t * (LANES // rank), cells, species, rank)
        core[:, lanes] = strip[...]
        for d, out in enumerate(outs):
            part = near + ((place[0] ^ d) & (half - 1))
            for y in range(share):
                out[y, :, lanes] = strip[pl.ds(part * share + y, step, stride=y_cells), :]


def contract(place, unfolded, basis, x_cells, y_cells, species, x_parts):
    rows, z = unfolded.shape
    rank = basis.shape[0]
    steps = 4
    block, cells = rows // steps, rows // species // steps
    width = species * rank
    share = y_cells // x_parts
    pieces = x_parts // 2
    return pl.pallas_call(
        functools.partial(core_kernel, species, y_cells),
        grid=(steps,),
        out_shape=[jax.ShapeDtypeStruct((rows // species, width), F32)]
        + [jax.ShapeDtypeStruct((share, x_cells, width), F32)] * pieces,
        in_specs=[
            SMEM,
            VMEM,
            pl.BlockSpec((rank, z), lambda i: (0, 0)),
        ],
        out_specs=[pl.BlockSpec((cells, width), lambda i: (i, 0))]
        + [pl.BlockSpec((share, x_cells // steps, width), lambda i: (0, i, 0))] * pieces,
        scratch_shapes=[
            pltpu.VMEM((2 * z, 2 * LANES), BF16),
            pltpu.VMEM((block, LANES), F32),
            pltpu.VMEM((cells, LANES), F32),
        ],
        compiler_params=SMALL,
        cost_estimate=pl.CostEstimate(flops=1 << 31, bytes_accessed=1 << 24, transcendentals=0),
        name="core",
    )(place, unfolded, basis)


def product_kernel(near_count, place, factor, *refs):
    near, far, (out, turn) = refs[:near_count], refs[near_count:-2], refs[-2:]
    share, size, width = near[0].shape
    rank = factor.shape[0]
    turn[...] = jnp.zeros_like(turn)
    for part, value in enumerate(in_two(factor[...])):
        for side in range(2):
            for q in range(LANES // rank):
                turn[
                    part * LANES + q * rank : part * LANES + (q + 1) * rank,
                    side * LANES + q * rank : side * LANES + (q + 1) * rank,
                ] = value
    strips = [
        piece[y, :, t : t + LANES]
        for piece in far
        for y in range(piece.shape[0])
        for t in range(0, width, LANES)
    ]
    both = jnp.concatenate(in_two(jnp.concatenate(strips, axis=0)), axis=1)
    turned = lax.dot_general(both, turn[...], ROWS_BY_ROWS, preferred_element_type=F32)
    turned = turned[:, :LANES] + turned[:, LANES:]
    count = width // LANES
    square = cross = 0.0
    for y in range(share):
        rows = [piece[y] for piece in near]
        for d in range(near_count):
            at = (d * share + y) * count
            rows.append(
                jnp.concatenate([turned[(at + t) * size : (at + t + 1) * size] for t in range(count)], axis=1)
            )
        high, low = in_two(jnp.concatenate(rows, axis=0))
        square = square + lax.dot_general(high, high, ROWS_BY_ROWS, preferred_element_type=F32)
        cross = cross + lax.dot_general(high, low, ROWS_BY_ROWS, preferred_element_type=F32)
    total = square + (cross + cross.T)
    for bit in bits(2 * near_count):
        step = size * bit
        swap = place[0] & bit != 0
        for axis in (0, 1):
            parts = [lax.slice_in_dim(total, c, c + step, axis=axis) for c in range(0, total.shape[axis], step)]
            swapped = jnp.concatenate([parts[c ^ 1] for c in range(len(parts))], axis=axis)
            total = jnp.where(swap, swapped, total)
    fold, upper, diagonal = folded(total)
    half = fold.shape[0]
    out[:half] = jnp.concatenate([fold, upper], axis=1)
    out[half:] = jnp.broadcast_to(jnp.concatenate([diagonal, diagonal], axis=1), (SUBLANES, 2 * half))


def product(place, factor, near, far):
    n = 2 * len(near) * near[0].shape[1]
    return pl.pallas_call(
        functools.partial(product_kernel, len(near)),
        out_shape=jax.ShapeDtypeStruct((n // 2 + SUBLANES, n), F32),
        in_specs=[SMEM] + [VMEM] * (1 + len(near) + len(far)),
        out_specs=VMEM,
        scratch_shapes=[pltpu.VMEM((2 * LANES, 2 * LANES), BF16)],
        compiler_params=SMALL,
        name="product",
    )(place, factor, *near, *far)


def triangle_kernel(scale, gram, out):
    half = gram.shape[1] // 2
    full = opened(gram[:half, :half], gram[:half, half:], gram[half : half + 1, :half])
    upper = joined(eliminated(tiles(full), [[] for _ in range(0, 2 * half, SUBLANES)])[0])
    r, c = triangle_ids(2 * half)
    out[...] = jnp.where(c >= r, upper * scale, 0.0)


def triangle(gram, scale):
    n = gram.shape[1]
    return pl.pallas_call(
        functools.partial(triangle_kernel, scale),
        out_shape=jax.ShapeDtypeStruct((n, n), F32),
        in_specs=[VMEM],
        out_specs=VMEM,
        compiler_params=SMALL,
        name="triangle",
    )(gram)


def local(state_field, start_basis):
    x_cells, y_cells, species, z_cells = state_field.shape
    rank_kept = start_basis.shape[1]
    unfolded = state_field.reshape(x_cells * y_cells * species, z_cells)
    x_parts = lax.axis_size("gx")
    place = lax.axis_index("gx").astype(jnp.int32).reshape(1)
    mine, other, held = local_gram(place, pltpu.with_memory_space_constraint(unfolded, pltpu.HBM))
    mine = summed(mine + partner(other, 1))
    other = partner(mine, 1)
    basis, image, gram = begin(place, mine, other, start_basis.T)
    far = []
    share = y_cells // x_parts
    for d, skip, count in far_pieces(x_parts, share):
        piece = contract_ahead(place, held, image, x_cells, y_cells, species, share, d, skip, count)
        far.append(partner(piece, d))
    basis_rows, basis, factor = finish(basis, gram)
    core_tensor, *near = contract(place, held, basis, x_cells, y_cells, species, x_parts)
    near = [partner(piece, d) if d else piece for d, piece in enumerate(near)]
    gram_x = product(place, factor, near, far)
    gram_x = summed(gram_x + partner(gram_x, 1))
    column_count = y_cells * lax.axis_size("gy") * species * rank_kept
    x_triangle = triangle(gram_x, 1.0 / column_count**0.5)
    return (core_tensor.reshape(x_cells, y_cells, species * rank_kept), basis_rows.T, x_triangle)


def far_pieces(x_parts, share):
    return [(d, 0, share) for d in range(x_parts // 2, x_parts)]


def solution(mesh):
    return jax.shard_map(
        local,
        mesh=mesh,
        in_specs=(P("gx", "gy", None, None), P()),
        out_specs=(P("gx", "gy", None), P(), P()),
        check_vma=False,
    )
```

profile of v0, /device:TPU:0, one launch (start us, length us, event | category | flops | bytes accessed | tf_op | source)
XLA Modules:
  0.0 75.8 jit_solution(15732839623442822409)
XLA Ops:
  0.6 0.0 copy-start
  0.6 5.0 %gram.1 = (f32[136,128]{1,0:T(8,128)S(1)}, f32[136,128]{1,0:T(8,128)S(1)}, f32[8192,256]{1,0:T(8,128)S(1)}) custom-call(s32[1]{0:T(128)} %bitcast.place, f32[8192,256]{1,0:T(8,128)} %bitcast.9), custom_call_target="tpu_custom_call" | custom-call | tf_op jit(solution)/shard_map/gram/pallas_call | solution.py:210
  5.6 0.6 collective-permute-start
  6.2 0.9 %collective-permute-done = f32[136,128]{1,0:T(8,128)S(1)} collective-permute-done((f32[136,128]{1,0:T(8,128)S(1)}, f32[136,128]{1,0:T(8,128)S(1)}, u32[]{:S(2)}, u32[]{:S(2)}) %collective-permute-start) | collective-permute-done | bytes 69664 | tf_op jit(solution)/shard_map/ppermute | solution.py:33
  7.1 3.8 %collective-permute-start.3 = (f32[136,128]{1,0:T(8,128)S(1)}, f32[136,128]{1,0:T(8,128)S(1)}, u32[]{:S(2)}, u32[]{:S(2)}) collective-permute-start(f32[136,128]{1,0:T(8,128)S(1)} %add.42), channel_id=1, source_target_pairs={{0,17},{1,16},{2,19},{3,18},{4,21},{5,20},{6,23},{7,22},{8,25},{9,... | collective-permute-start | bytes 208904 | tf_op jit(solution)/shard_map/ppermute | solution.py:33
  11.0 0.5 collective-permute-start.2
  11.5 0.1 collective-permute-start.1
  11.6 1.9 %collective-permute-done.3 = f32[136,128]{1,0:T(8,128)S(1)} collective-permute-done((f32[136,128]{1,0:T(8,128)S(1)}, f32[136,128]{1,0:T(8,128)S(1)}, u32[]{:S(2)}, u32[]{:S(2)}) %collective-permute-start.3) | collective-permute-done | bytes 69664 | tf_op jit(solution)/shard_map/ppermute | solution.py:33
  13.5 1.8 %collective-permute-done.2 = f32[136,128]{1,0:T(8,128)S(1)} collective-permute-done((f32[136,128]{1,0:T(8,128)S(1)}, f32[136,128]{1,0:T(8,128)S(1)}, u32[]{:S(2)}, u32[]{:S(2)}) %collective-permute-start.2) | collective-permute-done | bytes 69664 | tf_op jit(solution)/shard_map/ppermute | solution.py:33
  15.3 0.5 collective-permute-done.1
  15.8 3.7 %collective-permute-start.6 = (f32[136,128]{1,0:T(8,128)S(1)}, f32[136,128]{1,0:T(8,128)S(1)}, u32[]{:S(2)}, u32[]{:S(2)}) collective-permute-start(f32[136,128]{1,0:T(8,128)S(1)} %add_add_fusion.1), channel_id=1, source_target_pairs={{0,6},{1,7},{2,4},{3,5},{4,2},{5,3},{6,0},{7,1},{8,14},{9,15},{10,... | collective-permute-start | bytes 208904 | tf_op jit(solution)/shard_map/ppermute | solution.py:33
  19.5 0.0 collective-permute-start.5
  19.5 0.8 %collective-permute-start.4 = (f32[136,128]{1,0:T(8,128)S(1)}, f32[136,128]{1,0:T(8,128)S(1)}, u32[]{:S(2)}, u32[]{:S(2)}) collective-permute-start(f32[136,128]{1,0:T(8,128)S(1)} %add_add_fusion.1), channel_id=1, source_target_pairs={{0,2},{1,3},{2,0},{3,1},{4,6},{5,7},{6,4},{7,5},{8,10},{9,11},{10,... | collective-permute-start | bytes 208904 | tf_op jit(solution)/shard_map/ppermute | solution.py:33
  20.3 1.9 %collective-permute-done.6 = f32[136,128]{1,0:T(8,128)S(1)} collective-permute-done((f32[136,128]{1,0:T(8,128)S(1)}, f32[136,128]{1,0:T(8,128)S(1)}, u32[]{:S(2)}, u32[]{:S(2)}) %collective-permute-start.6) | collective-permute-done | bytes 69664 | tf_op jit(solution)/shard_map/ppermute | solution.py:33
  22.1 2.8 %collective-permute-done.5 = f32[136,128]{1,0:T(8,128)S(1)} collective-permute-done((f32[136,128]{1,0:T(8,128)S(1)}, f32[136,128]{1,0:T(8,128)S(1)}, u32[]{:S(2)}, u32[]{:S(2)}) %collective-permute-start.5) | collective-permute-done | bytes 69664 | tf_op jit(solution)/shard_map/ppermute | solution.py:33
  24.9 0.0 collective-permute-done.4
  24.9 0.1 collective-permute-start.7
  25.0 1.2 %collective-permute-done.7.other = f32[136,128]{1,0:T(8,128)S(1)} collective-permute-done((f32[136,128]{1,0:T(8,128)S(1)}, f32[136,128]{1,0:T(8,128)S(1)}, u32[]{:S(2)}, u32[]{:S(2)}) %collective-permute-start.7) | collective-permute-done | bytes 69664 | tf_op jit(solution)/shard_map/ppermute | solution.py:33
  26.3 0.0 copy-done
  26.3 3.5 %begin.1 = (f32[32,256]{1,0:T(8,128)S(1)}, f32[32,256]{1,0:T(8,128)S(1)}, f32[256,256]{1,0:T(8,128)S(1)}) custom-call(s32[1]{0:T(128)} %bitcast.place, f32[136,128]{1,0:T(8,128)S(1)} %add_add_fusion.mine, f32[136,128]{1,0:T(8,128)S(1)} %collective-permute-done.7.other, f32[32,256]{1,0:T(8,128)S(1)} %bitcast.8), custom_call_target="tpu_custom_call" | custom-call | tf_op jit(solution)/shard_map/begin/pallas_call | solution.py:248
  29.8 1.6 %shard_map.50 = f32[4,32,512]{2,1,0:T(8,128)S(1)} custom-call(s32[1]{0:T(128)} %bitcast.place, f32[32,256,256]{2,1,0:T(8,128)S(1)} %bitcast.6, f32[32,256]{1,0:T(8,128)S(1)} %get-tuple-element.26.image), custom_call_target="tpu_custom_call" | custom-call | flops 1073741824 | bytes 4194304 | tf_op jit(solution)/shard_map/pallas_call | solution.py:300
  31.3 1.6 %shard_map.49 = f32[4,32,512]{2,1,0:T(8,128)S(1)} custom-call(s32[1]{0:T(128)} %bitcast.place, f32[32,256,256]{2,1,0:T(8,128)S(1)} %bitcast.7, f32[32,256]{1,0:T(8,128)S(1)} %get-tuple-element.26.image), custom_call_target="tpu_custom_call" | custom-call | flops 1073741824 | bytes 4194304 | tf_op jit(solution)/shard_map/pallas_call | solution.py:300
  32.9 3.5 %finish.1 = (f32[32,256]{1,0:T(8,128)}, f32[32,256]{1,0:T(8,128)S(1)}, f32[32,32]{1,0:T(8,128)S(1)}) custom-call(f32[32,256]{1,0:T(8,128)S(1)} %get-tuple-element.18.basis, f32[256,256]{1,0:T(8,128)S(1)} %get-tuple-element.19.gram), custom_call_target="tpu_custom_call" | custom-call | flops 1073741824 | bytes 16777216 | tf_op jit(solution)/shard_map/finish/pallas_call | solution.py:272
  36.4 4.4 %core.1 = (f32[512,512]{1,0:T(8,128)}, f32[4,32,512]{2,1,0:T(8,128)S(1)}, f32[4,32,512]{2,1,0:T(8,128)S(1)}) custom-call(s32[1]{0:T(128)} %bitcast.place, f32[8192,256]{1,0:T(8,128)S(1)} %get-tuple-element.15.field, f32[32,256]{1,0:T(8,128)S(1)} %get-tuple-element.20.basis), custom_call_target="tpu_custom_call" | custom-call | flops 2147483648 | bytes 16777216 | tf_op jit(solution)/shard_map/core/pallas_call | solution.py:343
  40.9 0.2 collective-permute-start.8
  41.0 1.5 %collective-permute-start.9 = (f32[4,32,512]{2,1,0:T(8,128)S(1)}, f32[4,32,512]{2,1,0:T(8,128)S(1)}, u32[]{:S(2)}, u32[]{:S(2)}) collective-permute-start(f32[4,32,512]{2,1,0:T(8,128)S(1)} %shard_map.49), channel_id=1, source_target_pairs={{0,16},{1,17},{2,18},{3,19},{4,20},{5,21},{6,22},{7,23},{8,24},{9,... | collective-permute-start | bytes 786440 | tf_op jit(solution)/shard_map/ppermute | solution.py:33
  42.5 0.2 collective-permute-start.10
  42.7 0.0 collective-permute-done.8.refs_1_
  42.7 7.5 %collective-permute-done.9.refs_2_ = f32[4,32,512]{2,1,0:T(8,128)S(1)} collective-permute-done((f32[4,32,512]{2,1,0:T(8,128)S(1)}, f32[4,32,512]{2,1,0:T(8,128)S(1)}, u32[]{:S(2)}, u32[]{:S(2)}) %collective-permute-start.9) | collective-permute-done | bytes 262176 | tf_op jit(solution)/shard_map/ppermute | solution.py:33
  50.2 4.4 %collective-permute-done.10.refs_3_ = f32[4,32,512]{2,1,0:T(8,128)S(1)} collective-permute-done((f32[4,32,512]{2,1,0:T(8,128)S(1)}, f32[4,32,512]{2,1,0:T(8,128)S(1)}, u32[]{:S(2)}, u32[]{:S(2)}) %collective-permute-start.10) | collective-permute-done | bytes 262176 | tf_op jit(solution)/shard_map/ppermute | solution.py:33
  54.6 1.4 %product.1 = f32[72,128]{1,0:T(8,128)S(1)} custom-call(s32[1]{0:T(128)} %bitcast.place, f32[32,32]{1,0:T(8,128)S(1)} %get-tuple-element.23.factor, f32[4,32,512]{2,1,0:T(8,128)S(1)} %get-tuple-element.24.refs_0_, f32[4,32,512]{2,1,0:T(8,128)S(1)} %collective-permute-done.8.refs_1_, f32[4,32,512]{2,1,0:T(8,128)S(1)} %collective-permute-done.9.refs_2_, ...), custom_call_target="tpu_custom_call" | custom-call | tf_op jit(solution)/shard_map/product/pallas_call | solution.py:415
  56.0 0.4 collective-permute-start.11
  56.4 0.9 %collective-permute-done.11 = f32[72,128]{1,0:T(8,128)S(1)} collective-permute-done((f32[72,128]{1,0:T(8,128)S(1)}, f32[72,128]{1,0:T(8,128)S(1)}, u32[]{:S(2)}, u32[]{:S(2)}) %collective-permute-start.11) | collective-permute-done | bytes 36896 | tf_op jit(solution)/shard_map/ppermute | solution.py:33
  57.3 1.5 %collective-permute-start.14 = (f32[72,128]{1,0:T(8,128)S(1)}, f32[72,128]{1,0:T(8,128)S(1)}, u32[]{:S(2)}, u32[]{:S(2)}) collective-permute-start(f32[72,128]{1,0:T(8,128)S(1)} %add.49), channel_id=1, source_target_pairs={{0,17},{1,16},{2,19},{3,18},{4,21},{5,20},{6,23},{7,22},{8,25},{9,... | collective-permute-start | bytes 110600 | tf_op jit(solution)/shard_map/ppermute | solution.py:33
  58.8 1.5 %collective-permute-start.13 = (f32[72,128]{1,0:T(8,128)S(1)}, f32[72,128]{1,0:T(8,128)S(1)}, u32[]{:S(2)}, u32[]{:S(2)}) collective-permute-start(f32[72,128]{1,0:T(8,128)S(1)} %add.49), channel_id=1, source_target_pairs={{0,1},{1,0},{2,3},{3,2},{4,5},{5,4},{6,7},{7,6},{8,9},{9,8},{10,11... | collective-permute-start | bytes 110600 | tf_op jit(solution)/shard_map/ppermute | solution.py:33
  60.3 0.5 collective-permute-start.12
  60.8 1.4 %collective-permute-done.14 = f32[72,128]{1,0:T(8,128)S(1)} collective-permute-done((f32[72,128]{1,0:T(8,128)S(1)}, f32[72,128]{1,0:T(8,128)S(1)}, u32[]{:S(2)}, u32[]{:S(2)}) %collective-permute-start.14) | collective-permute-done | bytes 36896 | tf_op jit(solution)/shard_map/ppermute | solution.py:33
  62.2 0.6 collective-permute-done.13
  62.8 1.5 %collective-permute-done.12 = f32[72,128]{1,0:T(8,128)S(1)} collective-permute-done((f32[72,128]{1,0:T(8,128)S(1)}, f32[72,128]{1,0:T(8,128)S(1)}, u32[]{:S(2)}, u32[]{:S(2)}) %collective-permute-start.12) | collective-permute-done | bytes 36896 | tf_op jit(solution)/shard_map/ppermute | solution.py:33
  64.3 2.7 %collective-permute-start.17 = (f32[72,128]{1,0:T(8,128)S(1)}, f32[72,128]{1,0:T(8,128)S(1)}, u32[]{:S(2)}, u32[]{:S(2)}) collective-permute-start(f32[72,128]{1,0:T(8,128)S(1)} %add_add_fusion.3), channel_id=1, source_target_pairs={{0,6},{1,7},{2,4},{3,5},{4,2},{5,3},{6,0},{7,1},{8,14},{9,15},{10,... | collective-permute-start | bytes 110600 | tf_op jit(solution)/shard_map/ppermute | solution.py:33
  67.0 0.0 collective-permute-start.16
  67.0 1.7 %collective-permute-start.15 = (f32[72,128]{1,0:T(8,128)S(1)}, f32[72,128]{1,0:T(8,128)S(1)}, u32[]{:S(2)}, u32[]{:S(2)}) collective-permute-start(f32[72,128]{1,0:T(8,128)S(1)} %add_add_fusion.3), channel_id=1, source_target_pairs={{0,2},{1,3},{2,0},{3,1},{4,6},{5,7},{6,4},{7,5},{8,10},{9,11},{10,... | collective-permute-start | bytes 110600 | tf_op jit(solution)/shard_map/ppermute | solution.py:33
  68.7 1.4 %collective-permute-done.17 = f32[72,128]{1,0:T(8,128)S(1)} collective-permute-done((f32[72,128]{1,0:T(8,128)S(1)}, f32[72,128]{1,0:T(8,128)S(1)}, u32[]{:S(2)}, u32[]{:S(2)}) %collective-permute-start.17) | collective-permute-done | bytes 36896 | tf_op jit(solution)/shard_map/ppermute | solution.py:33
  70.2 1.7 %collective-permute-done.16 = f32[72,128]{1,0:T(8,128)S(1)} collective-permute-done((f32[72,128]{1,0:T(8,128)S(1)}, f32[72,128]{1,0:T(8,128)S(1)}, u32[]{:S(2)}, u32[]{:S(2)}) %collective-permute-start.16) | collective-permute-done | bytes 36896 | tf_op jit(solution)/shard_map/ppermute | solution.py:33
  71.8 0.0 collective-permute-done.15
  71.8 3.9 %triangle.1 = f32[128,128]{1,0:T(8,128)} custom-call(f32[72,128]{1,0:T(8,128)S(1)} %add_add_fusion.2.gram), custom_call_target="tpu_custom_call" | custom-call | tf_op jit(solution)/shard_map/triangle/pallas_call | solution.py:436
  (6 shorter events, 0.1 us)
Async XLA Ops:
  0.6 25.6 %copy-start = (f32[256,32]{0,1:T(8,128)S(1)}, f32[256,32]{0,1:T(8,128)}, u32[]{:S(2)}) copy-start(f32[256,32]{0,1:T(8,128)} %param.3) | copy-start | bytes 98308
  5.6 1.5 %collective-permute-start = (f32[136,128]{1,0:T(8,128)S(1)}, f32[136,128]{1,0:T(8,128)S(1)}, u32[]{:S(2)}, u32[]{:S(2)}) collective-permute-start(f32[136,128]{1,0:T(8,128)S(1)} %get-tuple-element.17), channel_id=1, source_target_pairs={{0,8},{1,9},{2,10},{3,11},{4,12},{5,13},{6,14},{7,15},{8,0},{9,1},... | collective-permute-start | bytes 208904 | tf_op jit(solution)/shard_map/ppermute | solution.py:33
  7.1 6.3 %collective-permute-start.3 = (f32[136,128]{1,0:T(8,128)S(1)}, f32[136,128]{1,0:T(8,128)S(1)}, u32[]{:S(2)}, u32[]{:S(2)}) collective-permute-start(f32[136,128]{1,0:T(8,128)S(1)} %add.42), channel_id=1, source_target_pairs={{0,17},{1,16},{2,19},{3,18},{4,21},{5,20},{6,23},{7,22},{8,25},{9,... | collective-permute-start | bytes 208904 | tf_op jit(solution)/shard_map/ppermute | solution.py:33
  11.0 4.3 %collective-permute-start.2 = (f32[136,128]{1,0:T(8,128)S(1)}, f32[136,128]{1,0:T(8,128)S(1)}, u32[]{:S(2)}, u32[]{:S(2)}) collective-permute-start(f32[136,128]{1,0:T(8,128)S(1)} %add.42), channel_id=1, source_target_pairs={{0,1},{1,0},{2,3},{3,2},{4,5},{5,4},{6,7},{7,6},{8,9},{9,8},{10,11... | collective-permute-start | bytes 208904 | tf_op jit(solution)/shard_map/ppermute | solution.py:33
  11.5 4.3 %collective-permute-start.1 = (f32[136,128]{1,0:T(8,128)S(1)}, f32[136,128]{1,0:T(8,128)S(1)}, u32[]{:S(2)}, u32[]{:S(2)}) collective-permute-start(f32[136,128]{1,0:T(8,128)S(1)} %add.42), channel_id=1, source_target_pairs={{0,16},{1,17},{2,18},{3,19},{4,20},{5,21},{6,22},{7,23},{8,24},{9,... | collective-permute-start | bytes 208904 | tf_op jit(solution)/shard_map/ppermute | solution.py:33
  15.8 6.3 %collective-permute-start.6 = (f32[136,128]{1,0:T(8,128)S(1)}, f32[136,128]{1,0:T(8,128)S(1)}, u32[]{:S(2)}, u32[]{:S(2)}) collective-permute-start(f32[136,128]{1,0:T(8,128)S(1)} %add_add_fusion.1), channel_id=1, source_target_pairs={{0,6},{1,7},{2,4},{3,5},{4,2},{5,3},{6,0},{7,1},{8,14},{9,15},{10,... | collective-permute-start | bytes 208904 | tf_op jit(solution)/shard_map/ppermute | solution.py:33
  19.5 5.5 %collective-permute-start.5 = (f32[136,128]{1,0:T(8,128)S(1)}, f32[136,128]{1,0:T(8,128)S(1)}, u32[]{:S(2)}, u32[]{:S(2)}) collective-permute-start(f32[136,128]{1,0:T(8,128)S(1)} %add_add_fusion.1), channel_id=1, source_target_pairs={{0,4},{1,5},{2,6},{3,7},{4,0},{5,1},{6,2},{7,3},{8,12},{9,13},{10,... | collective-permute-start | bytes 208904 | tf_op jit(solution)/shard_map/ppermute | solution.py:33
  19.5 5.5 %collective-permute-start.4 = (f32[136,128]{1,0:T(8,128)S(1)}, f32[136,128]{1,0:T(8,128)S(1)}, u32[]{:S(2)}, u32[]{:S(2)}) collective-permute-start(f32[136,128]{1,0:T(8,128)S(1)} %add_add_fusion.1), channel_id=1, source_target_pairs={{0,2},{1,3},{2,0},{3,1},{4,6},{5,7},{6,4},{7,5},{8,10},{9,11},{10,... | collective-permute-start | bytes 208904 | tf_op jit(solution)/shard_map/ppermute | solution.py:33
  24.9 1.3 %collective-permute-start.7 = (f32[136,128]{1,0:T(8,128)S(1)}, f32[136,128]{1,0:T(8,128)S(1)}, u32[]{:S(2)}, u32[]{:S(2)}) collective-permute-start(f32[136,128]{1,0:T(8,128)S(1)} %add_add_fusion.mine), channel_id=1, source_target_pairs={{0,8},{1,9},{2,10},{3,11},{4,12},{5,13},{6,14},{7,15},{8,0},{9,1},... | collective-permute-start | bytes 208904 | tf_op jit(solution)/shard_map/ppermute | solution.py:33
  40.9 1.9 %collective-permute-start.8 = (f32[4,32,512]{2,1,0:T(8,128)S(1)}, f32[4,32,512]{2,1,0:T(8,128)S(1)}, u32[]{:S(2)}, u32[]{:S(2)}) collective-permute-start(f32[4,32,512]{2,1,0:T(8,128)S(1)} %get-tuple-element.25), channel_id=1, source_target_pairs={{0,8},{1,9},{2,10},{3,11},{4,12},{5,13},{6,14},{7,15},{8,0},{9,1},... | collective-permute-start | bytes 786440 | tf_op jit(solution)/shard_map/ppermute | solution.py:33
  41.0 9.2 %collective-permute-start.9 = (f32[4,32,512]{2,1,0:T(8,128)S(1)}, f32[4,32,512]{2,1,0:T(8,128)S(1)}, u32[]{:S(2)}, u32[]{:S(2)}) collective-permute-start(f32[4,32,512]{2,1,0:T(8,128)S(1)} %shard_map.49), channel_id=1, source_target_pairs={{0,16},{1,17},{2,18},{3,19},{4,20},{5,21},{6,22},{7,23},{8,24},{9,... | collective-permute-start | bytes 786440 | tf_op jit(solution)/shard_map/ppermute | solution.py:33
  42.5 12.0 %collective-permute-start.10 = (f32[4,32,512]{2,1,0:T(8,128)S(1)}, f32[4,32,512]{2,1,0:T(8,128)S(1)}, u32[]{:S(2)}, u32[]{:S(2)}) collective-permute-start(f32[4,32,512]{2,1,0:T(8,128)S(1)} %shard_map.50), channel_id=1, source_target_pairs={{0,24},{1,25},{2,26},{3,27},{4,28},{5,29},{6,30},{7,31},{8,16},{9,... | collective-permute-start | bytes 786440 | tf_op jit(solution)/shard_map/ppermute | solution.py:33
  56.0 1.3 %collective-permute-start.11 = (f32[72,128]{1,0:T(8,128)S(1)}, f32[72,128]{1,0:T(8,128)S(1)}, u32[]{:S(2)}, u32[]{:S(2)}) collective-permute-start(f32[72,128]{1,0:T(8,128)S(1)} %product.1), channel_id=1, source_target_pairs={{0,8},{1,9},{2,10},{3,11},{4,12},{5,13},{6,14},{7,15},{8,0},{9,1},... | collective-permute-start | bytes 110600 | tf_op jit(solution)/shard_map/ppermute | solution.py:33
  57.3 4.9 %collective-permute-start.14 = (f32[72,128]{1,0:T(8,128)S(1)}, f32[72,128]{1,0:T(8,128)S(1)}, u32[]{:S(2)}, u32[]{:S(2)}) collective-permute-start(f32[72,128]{1,0:T(8,128)S(1)} %add.49), channel_id=1, source_target_pairs={{0,17},{1,16},{2,19},{3,18},{4,21},{5,20},{6,23},{7,22},{8,25},{9,... | collective-permute-start | bytes 110600 | tf_op jit(solution)/shard_map/ppermute | solution.py:33
  58.8 4.0 %collective-permute-start.13 = (f32[72,128]{1,0:T(8,128)S(1)}, f32[72,128]{1,0:T(8,128)S(1)}, u32[]{:S(2)}, u32[]{:S(2)}) collective-permute-start(f32[72,128]{1,0:T(8,128)S(1)} %add.49), channel_id=1, source_target_pairs={{0,1},{1,0},{2,3},{3,2},{4,5},{5,4},{6,7},{7,6},{8,9},{9,8},{10,11... | collective-permute-start | bytes 110600 | tf_op jit(solution)/shard_map/ppermute | solution.py:33
  60.3 4.0 %collective-permute-start.12 = (f32[72,128]{1,0:T(8,128)S(1)}, f32[72,128]{1,0:T(8,128)S(1)}, u32[]{:S(2)}, u32[]{:S(2)}) collective-permute-start(f32[72,128]{1,0:T(8,128)S(1)} %add.49), channel_id=1, source_target_pairs={{0,16},{1,17},{2,18},{3,19},{4,20},{5,21},{6,22},{7,23},{8,24},{9,... | collective-permute-start | bytes 110600 | tf_op jit(solution)/shard_map/ppermute | solution.py:33
  64.3 5.9 %collective-permute-start.17 = (f32[72,128]{1,0:T(8,128)S(1)}, f32[72,128]{1,0:T(8,128)S(1)}, u32[]{:S(2)}, u32[]{:S(2)}) collective-permute-start(f32[72,128]{1,0:T(8,128)S(1)} %add_add_fusion.3), channel_id=1, source_target_pairs={{0,6},{1,7},{2,4},{3,5},{4,2},{5,3},{6,0},{7,1},{8,14},{9,15},{10,... | collective-permute-start | bytes 110600 | tf_op jit(solution)/shard_map/ppermute | solution.py:33
  67.0 4.9 %collective-permute-start.16 = (f32[72,128]{1,0:T(8,128)S(1)}, f32[72,128]{1,0:T(8,128)S(1)}, u32[]{:S(2)}, u32[]{:S(2)}) collective-permute-start(f32[72,128]{1,0:T(8,128)S(1)} %add_add_fusion.3), channel_id=1, source_target_pairs={{0,4},{1,5},{2,6},{3,7},{4,0},{5,1},{6,2},{7,3},{8,12},{9,13},{10,... | collective-permute-start | bytes 110600 | tf_op jit(solution)/shard_map/ppermute | solution.py:33
  67.0 4.9 %collective-permute-start.15 = (f32[72,128]{1,0:T(8,128)S(1)}, f32[72,128]{1,0:T(8,128)S(1)}, u32[]{:S(2)}, u32[]{:S(2)}) collective-permute-start(f32[72,128]{1,0:T(8,128)S(1)} %add_add_fusion.3), channel_id=1, source_target_pairs={{0,2},{1,3},{2,0},{3,1},{4,6},{5,7},{6,4},{7,5},{8,10},{9,11},{10,... | collective-permute-start | bytes 110600 | tf_op jit(solution)/shard_map/ppermute | solution.py:33
where the time goes:
time: 75.9 us; the launch traced here: 75.8 us
  waiting for transfers between devices  30.3 us (40%)
  Pallas kernels  24.9 us (33%)
  starting transfers between devices  19.8 us (26%)
    ppermute x18, waiting for transfers between devices, partner(): return lax.ppermute(value, ('gx', 'gy'), pairs)  30.3 us
    ppermute x18, starting transfers between devices, partner(): return lax.ppermute(value, ('gx', 'gy'), pairs)  19.8 us
    pallas_call x1, Pallas kernels, local_gram(): pl.pallas_call(functools.partial(gram_kernel, cuts), out_shape=[out, out,...  4.99 us
    pallas_call x1, Pallas kernels, contract(): pl.pallas_call(functools.partial(core_kernel, species, y_cells), grid=(st...  4.43 us
    pallas_call x1, Pallas kernels, triangle(): pl.pallas_call(functools.partial(triangle_kernel, scale), out_shape=jax.S...  3.95 us
    pallas_call x1, Pallas kernels, finish(): pl.pallas_call(finish_kernel, out_shape=[jax.ShapeDtypeStruct((rank, z),...  3.52 us
    pallas_call x1, Pallas kernels, begin(): pl.pallas_call(begin_kernel, out_shape=[rows, rows, jax.ShapeDtypeStruct(...  3.5 us
    pallas_call x2, Pallas kernels, contract_ahead(): pl.pallas_call(functools.partial(ahead_kernel, d, share, skip, species),...  3.13 us
  transfers between devices with their start and end apart: 18, of which 15 were waited for; matrix products, arithmetic and copies ran while one was open for 0% of the time, Pallas kernels for 0%

commit v1 on v0

--- a/solution.py
+++ b/solution.py
@@ -177,12 +177,14 @@
     ]
     for copy in copies:
         copy.start()
-    square = cross = 0.0
+    total = 0.0
     for copy, a, b in zip(copies, cuts[:-1], cuts[1:]):
         copy.wait()
         high, low = in_two(held[a:b])
-        square = square + lax.dot_general(high, high, COLUMNS_BY_COLUMNS, preferred_element_type=F32)
-        cross = cross + lax.dot_general(high, low, COLUMNS_BY_COLUMNS, preferred_element_type=F32)
+        total = total + lax.dot_general(
+            high, jnp.concatenate([high, low], axis=1), COLUMNS_BY_COLUMNS, preferred_element_type=F32
+        )
+    square, cross = jnp.split(total, 2, axis=1)
     fold, upper, diagonal = folded(square + (cross + cross.T))
     half = fold.shape[0]
     edge = SUBLANES
@@ -385,7 +387,7 @@
     turned = lax.dot_general(both, turn[...], ROWS_BY_ROWS, preferred_element_type=F32)
     turned = turned[:, :LANES] + turned[:, LANES:]
     count = width // LANES
-    square = cross = 0.0
+    columns = []
     for y in range(share):
         rows = [piece[y] for piece in near]
         for d in range(near_count):
@@ -393,9 +395,12 @@
             rows.append(
                 jnp.concatenate([turned[(at + t) * size : (at + t + 1) * size] for t in range(count)], axis=1)
             )
-        high, low = in_two(jnp.concatenate(rows, axis=0))
-        square = square + lax.dot_general(high, high, ROWS_BY_ROWS, preferred_element_type=F32)
-        cross = cross + lax.dot_general(high, low, ROWS_BY_ROWS, preferred_element_type=F32)
+        columns.append(jnp.concatenate(rows, axis=0))
+    high, low = in_two(jnp.concatenate(columns, axis=1))
+    total = lax.dot_general(
+        high, jnp.concatenate([high, low], axis=0), ROWS_BY_ROWS, preferred_element_type=F32
+    )
+    square, cross = jnp.split(total, 2, axis=1)
     total = square + (cross + cross.T)
     for bit in bits(2 * near_count):
         step = size * bit

time: 75.9 us -> 75.9 us (level)
  no operation moved by 1% of the time
where the time goes in v1:
time: 75.9 us; the launch traced here: 75.8 us
  waiting for transfers between devices  30.3 us (40%)
  Pallas kernels  24.9 us (33%)
  starting transfers between devices  19.8 us (26%)
    ppermute x18, waiting for transfers between devices, partner(): return lax.ppermute(value, ('gx', 'gy'), pairs)  30.3 us
    ppermute x18, starting transfers between devices, partner(): return lax.ppermute(value, ('gx', 'gy'), pairs)  19.8 us
    pallas_call x1, Pallas kernels, local_gram(): pl.pallas_call(functools.partial(gram_kernel, cuts), out_shape=[out, out,...  4.99 us
    pallas_call x1, Pallas kernels, contract(): pl.pallas_call(functools.partial(core_kernel, species, y_cells), grid=(st...  4.43 us
    pallas_call x1, Pallas kernels, triangle(): pl.pallas_call(functools.partial(triangle_kernel, scale), out_shape=jax.S...  3.95 us
    pallas_call x1, Pallas kernels, finish(): pl.pallas_call(finish_kernel, out_shape=[jax.ShapeDtypeStruct((rank, z),...  3.52 us
    pallas_call x1, Pallas kernels, begin(): pl.pallas_call(begin_kernel, out_shape=[rows, rows, jax.ShapeDtypeStruct(...  3.5 us
    pallas_call x2, Pallas kernels, contract_ahead(): pl.pallas_call(functools.partial(ahead_kernel, d, share, skip, species),...  3.13 us
  transfers between devices with their start and end apart: 18, of which 15 were waited for; matrix products, arithmetic and copies ran while one was open for 0% of the time, Pallas kernels for 0%

profile of v1, /device:TPU:0, one launch (start us, length us, event | category | flops | bytes accessed | tf_op | source)
XLA Modules:
  0.0 75.8 jit_solution(16297188402200736809)
XLA Ops:
  0.6 0.0 copy-start
  0.6 5.0 %gram.1 = (f32[136,128]{1,0:T(8,128)S(1)}, f32[136,128]{1,0:T(8,128)S(1)}, f32[8192,256]{1,0:T(8,128)S(1)}) custom-call(s32[1]{0:T(128)} %bitcast.place, f32[8192,256]{1,0:T(8,128)} %bitcast.9), custom_call_target="tpu_custom_call" | custom-call | tf_op jit(solution)/shard_map/gram/pallas_call | solution.py:212
  5.6 0.6 collective-permute-start
  6.2 0.9 %collective-permute-done = f32[136,128]{1,0:T(8,128)S(1)} collective-permute-done((f32[136,128]{1,0:T(8,128)S(1)}, f32[136,128]{1,0:T(8,128)S(1)}, u32[]{:S(2)}, u32[]{:S(2)}) %collective-permute-start) | collective-permute-done | bytes 69664 | tf_op jit(solution)/shard_map/ppermute | solution.py:33
  7.1 3.8 %collective-permute-start.3 = (f32[136,128]{1,0:T(8,128)S(1)}, f32[136,128]{1,0:T(8,128)S(1)}, u32[]{:S(2)}, u32[]{:S(2)}) collective-permute-start(f32[136,128]{1,0:T(8,128)S(1)} %add.42), channel_id=1, source_target_pairs={{0,17},{1,16},{2,19},{3,18},{4,21},{5,20},{6,23},{7,22},{8,25},{9,... | collective-permute-start | bytes 208904 | tf_op jit(solution)/shard_map/ppermute | solution.py:33
  11.0 0.5 collective-permute-start.2
  11.5 0.1 collective-permute-start.1
  11.6 1.9 %collective-permute-done.3 = f32[136,128]{1,0:T(8,128)S(1)} collective-permute-done((f32[136,128]{1,0:T(8,128)S(1)}, f32[136,128]{1,0:T(8,128)S(1)}, u32[]{:S(2)}, u32[]{:S(2)}) %collective-permute-start.3) | collective-permute-done | bytes 69664 | tf_op jit(solution)/shard_map/ppermute | solution.py:33
  13.5 1.8 %collective-permute-done.2 = f32[136,128]{1,0:T(8,128)S(1)} collective-permute-done((f32[136,128]{1,0:T(8,128)S(1)}, f32[136,128]{1,0:T(8,128)S(1)}, u32[]{:S(2)}, u32[]{:S(2)}) %collective-permute-start.2) | collective-permute-done | bytes 69664 | tf_op jit(solution)/shard_map/ppermute | solution.py:33
  15.3 0.5 collective-permute-done.1
  15.8 3.7 %collective-permute-start.6 = (f32[136,128]{1,0:T(8,128)S(1)}, f32[136,128]{1,0:T(8,128)S(1)}, u32[]{:S(2)}, u32[]{:S(2)}) collective-permute-start(f32[136,128]{1,0:T(8,128)S(1)} %add_add_fusion.1), channel_id=1, source_target_pairs={{0,6},{1,7},{2,4},{3,5},{4,2},{5,3},{6,0},{7,1},{8,14},{9,15},{10,... | collective-permute-start | bytes 208904 | tf_op jit(solution)/shard_map/ppermute | solution.py:33
  19.5 0.0 collective-permute-start.5
  19.5 0.8 %collective-permute-start.4 = (f32[136,128]{1,0:T(8,128)S(1)}, f32[136,128]{1,0:T(8,128)S(1)}, u32[]{:S(2)}, u32[]{:S(2)}) collective-permute-start(f32[136,128]{1,0:T(8,128)S(1)} %add_add_fusion.1), channel_id=1, source_target_pairs={{0,2},{1,3},{2,0},{3,1},{4,6},{5,7},{6,4},{7,5},{8,10},{9,11},{10,... | collective-permute-start | bytes 208904 | tf_op jit(solution)/shard_map/ppermute | solution.py:33
  20.3 1.9 %collective-permute-done.6 = f32[136,128]{1,0:T(8,128)S(1)} collective-permute-done((f32[136,128]{1,0:T(8,128)S(1)}, f32[136,128]{1,0:T(8,128)S(1)}, u32[]{:S(2)}, u32[]{:S(2)}) %collective-permute-start.6) | collective-permute-done | bytes 69664 | tf_op jit(solution)/shard_map/ppermute | solution.py:33
  22.1 2.8 %collective-permute-done.5 = f32[136,128]{1,0:T(8,128)S(1)} collective-permute-done((f32[136,128]{1,0:T(8,128)S(1)}, f32[136,128]{1,0:T(8,128)S(1)}, u32[]{:S(2)}, u32[]{:S(2)}) %collective-permute-start.5) | collective-permute-done | bytes 69664 | tf_op jit(solution)/shard_map/ppermute | solution.py:33
  24.9 0.0 collective-permute-done.4
  24.9 0.1 collective-permute-start.7
  25.0 1.2 %collective-permute-done.7.other = f32[136,128]{1,0:T(8,128)S(1)} collective-permute-done((f32[136,128]{1,0:T(8,128)S(1)}, f32[136,128]{1,0:T(8,128)S(1)}, u32[]{:S(2)}, u32[]{:S(2)}) %collective-permute-start.7) | collective-permute-done | bytes 69664 | tf_op jit(solution)/shard_map/ppermute | solution.py:33
  26.3 0.0 copy-done
  26.3 3.5 %begin.1 = (f32[32,256]{1,0:T(8,128)S(1)}, f32[32,256]{1,0:T(8,128)S(1)}, f32[256,256]{1,0:T(8,128)S(1)}) custom-call(s32[1]{0:T(128)} %bitcast.place, f32[136,128]{1,0:T(8,128)S(1)} %add_add_fusion.mine, f32[136,128]{1,0:T(8,128)S(1)} %collective-permute-done.7.other, f32[32,256]{1,0:T(8,128)S(1)} %bitcast.8), custom_call_target="tpu_custom_call" | custom-call | tf_op jit(solution)/shard_map/begin/pallas_call | solution.py:250
  29.8 1.6 %shard_map.50 = f32[4,32,512]{2,1,0:T(8,128)S(1)} custom-call(s32[1]{0:T(128)} %bitcast.place, f32[32,256,256]{2,1,0:T(8,128)S(1)} %bitcast.6, f32[32,256]{1,0:T(8,128)S(1)} %get-tuple-element.26.image), custom_call_target="tpu_custom_call" | custom-call | flops 1073741824 | bytes 4194304 | tf_op jit(solution)/shard_map/pallas_call | solution.py:302
  31.3 1.6 %shard_map.49 = f32[4,32,512]{2,1,0:T(8,128)S(1)} custom-call(s32[1]{0:T(128)} %bitcast.place, f32[32,256,256]{2,1,0:T(8,128)S(1)} %bitcast.7, f32[32,256]{1,0:T(8,128)S(1)} %get-tuple-element.26.image), custom_call_target="tpu_custom_call" | custom-call | flops 1073741824 | bytes 4194304 | tf_op jit(solution)/shard_map/pallas_call | solution.py:302
  32.9 3.5 %finish.1 = (f32[32,256]{1,0:T(8,128)}, f32[32,256]{1,0:T(8,128)S(1)}, f32[32,32]{1,0:T(8,128)S(1)}) custom-call(f32[32,256]{1,0:T(8,128)S(1)} %get-tuple-element.18.basis, f32[256,256]{1,0:T(8,128)S(1)} %get-tuple-element.19.gram), custom_call_target="tpu_custom_call" | custom-call | flops 1073741824 | bytes 16777216 | tf_op jit(solution)/shard_map/finish/pallas_call | solution.py:274
  36.4 4.4 %core.1 = (f32[512,512]{1,0:T(8,128)}, f32[4,32,512]{2,1,0:T(8,128)S(1)}, f32[4,32,512]{2,1,0:T(8,128)S(1)}) custom-call(s32[1]{0:T(128)} %bitcast.place, f32[8192,256]{1,0:T(8,128)S(1)} %get-tuple-element.15.field, f32[32,256]{1,0:T(8,128)S(1)} %get-tuple-element.20.basis), custom_call_target="tpu_custom_call" | custom-call | flops 2147483648 | bytes 16777216 | tf_op jit(solution)/shard_map/core/pallas_call | solution.py:345
  40.9 0.2 collective-permute-start.8
  41.0 1.5 %collective-permute-start.9 = (f32[4,32,512]{2,1,0:T(8,128)S(1)}, f32[4,32,512]{2,1,0:T(8,128)S(1)}, u32[]{:S(2)}, u32[]{:S(2)}) collective-permute-start(f32[4,32,512]{2,1,0:T(8,128)S(1)} %shard_map.49), channel_id=1, source_target_pairs={{0,16},{1,17},{2,18},{3,19},{4,20},{5,21},{6,22},{7,23},{8,24},{9,... | collective-permute-start | bytes 786440 | tf_op jit(solution)/shard_map/ppermute | solution.py:33
  42.5 0.2 collective-permute-start.10
  42.7 0.0 collective-permute-done.8.refs_1_
  42.7 7.5 %collective-permute-done.9.refs_2_ = f32[4,32,512]{2,1,0:T(8,128)S(1)} collective-permute-done((f32[4,32,512]{2,1,0:T(8,128)S(1)}, f32[4,32,512]{2,1,0:T(8,128)S(1)}, u32[]{:S(2)}, u32[]{:S(2)}) %collective-permute-start.9) | collective-permute-done | bytes 262176 | tf_op jit(solution)/shard_map/ppermute | solution.py:33
  50.2 4.4 %collective-permute-done.10.refs_3_ = f32[4,32,512]{2,1,0:T(8,128)S(1)} collective-permute-done((f32[4,32,512]{2,1,0:T(8,128)S(1)}, f32[4,32,512]{2,1,0:T(8,128)S(1)}, u32[]{:S(2)}, u32[]{:S(2)}) %collective-permute-start.10) | collective-permute-done | bytes 262176 | tf_op jit(solution)/shard_map/ppermute | solution.py:33
  54.6 1.4 %product.1 = f32[72,128]{1,0:T(8,128)S(1)} custom-call(s32[1]{0:T(128)} %bitcast.place, f32[32,32]{1,0:T(8,128)S(1)} %get-tuple-element.23.factor, f32[4,32,512]{2,1,0:T(8,128)S(1)} %get-tuple-element.24.refs_0_, f32[4,32,512]{2,1,0:T(8,128)S(1)} %collective-permute-done.8.refs_1_, f32[4,32,512]{2,1,0:T(8,128)S(1)} %collective-permute-done.9.refs_2_, ...), custom_call_target="tpu_custom_call" | custom-call | tf_op jit(solution)/shard_map/product/pallas_call | solution.py:420
  56.0 0.4 collective-permute-start.11
  56.4 0.9 %collective-permute-done.11 = f32[72,128]{1,0:T(8,128)S(1)} collective-permute-done((f32[72,128]{1,0:T(8,128)S(1)}, f32[72,128]{1,0:T(8,128)S(1)}, u32[]{:S(2)}, u32[]{:S(2)}) %collective-permute-start.11) | collective-permute-done | bytes 36896 | tf_op jit(solution)/shard_map/ppermute | solution.py:33
  57.3 1.5 %collective-permute-start.14 = (f32[72,128]{1,0:T(8,128)S(1)}, f32[72,128]{1,0:T(8,128)S(1)}, u32[]{:S(2)}, u32[]{:S(2)}) collective-permute-start(f32[72,128]{1,0:T(8,128)S(1)} %add.49), channel_id=1, source_target_pairs={{0,17},{1,16},{2,19},{3,18},{4,21},{5,20},{6,23},{7,22},{8,25},{9,... | collective-permute-start | bytes 110600 | tf_op jit(solution)/shard_map/ppermute | solution.py:33
  58.8 1.5 %collective-permute-start.13 = (f32[72,128]{1,0:T(8,128)S(1)}, f32[72,128]{1,0:T(8,128)S(1)}, u32[]{:S(2)}, u32[]{:S(2)}) collective-permute-start(f32[72,128]{1,0:T(8,128)S(1)} %add.49), channel_id=1, source_target_pairs={{0,1},{1,0},{2,3},{3,2},{4,5},{5,4},{6,7},{7,6},{8,9},{9,8},{10,11... | collective-permute-start | bytes 110600 | tf_op jit(solution)/shard_map/ppermute | solution.py:33
  60.3 0.5 collective-permute-start.12
  60.8 1.4 %collective-permute-done.14 = f32[72,128]{1,0:T(8,128)S(1)} collective-permute-done((f32[72,128]{1,0:T(8,128)S(1)}, f32[72,128]{1,0:T(8,128)S(1)}, u32[]{:S(2)}, u32[]{:S(2)}) %collective-permute-start.14) | collective-permute-done | bytes 36896 | tf_op jit(solution)/shard_map/ppermute | solution.py:33
  62.1 0.6 collective-permute-done.13
  62.8 1.5 %collective-permute-done.12 = f32[72,128]{1,0:T(8,128)S(1)} collective-permute-done((f32[72,128]{1,0:T(8,128)S(1)}, f32[72,128]{1,0:T(8,128)S(1)}, u32[]{:S(2)}, u32[]{:S(2)}) %collective-permute-start.12) | collective-permute-done | bytes 36896 | tf_op jit(solution)/shard_map/ppermute | solution.py:33
  64.2 2.7 %collective-permute-start.17 = (f32[72,128]{1,0:T(8,128)S(1)}, f32[72,128]{1,0:T(8,128)S(1)}, u32[]{:S(2)}, u32[]{:S(2)}) collective-permute-start(f32[72,128]{1,0:T(8,128)S(1)} %add_add_fusion.3), channel_id=1, source_target_pairs={{0,6},{1,7},{2,4},{3,5},{4,2},{5,3},{6,0},{7,1},{8,14},{9,15},{10,... | collective-permute-start | bytes 110600 | tf_op jit(solution)/shard_map/ppermute | solution.py:33
  66.9 0.0 collective-permute-start.16
  66.9 1.7 %collective-permute-start.15 = (f32[72,128]{1,0:T(8,128)S(1)}, f32[72,128]{1,0:T(8,128)S(1)}, u32[]{:S(2)}, u32[]{:S(2)}) collective-permute-start(f32[72,128]{1,0:T(8,128)S(1)} %add_add_fusion.3), channel_id=1, source_target_pairs={{0,2},{1,3},{2,0},{3,1},{4,6},{5,7},{6,4},{7,5},{8,10},{9,11},{10,... | collective-permute-start | bytes 110600 | tf_op jit(solution)/shard_map/ppermute | solution.py:33
  68.7 1.4 %collective-permute-done.17 = f32[72,128]{1,0:T(8,128)S(1)} collective-permute-done((f32[72,128]{1,0:T(8,128)S(1)}, f32[72,128]{1,0:T(8,128)S(1)}, u32[]{:S(2)}, u32[]{:S(2)}) %collective-permute-start.17) | collective-permute-done | bytes 36896 | tf_op jit(solution)/shard_map/ppermute | solution.py:33
  70.1 1.7 %collective-permute-done.16 = f32[72,128]{1,0:T(8,128)S(1)} collective-permute-done((f32[72,128]{1,0:T(8,128)S(1)}, f32[72,128]{1,0:T(8,128)S(1)}, u32[]{:S(2)}, u32[]{:S(2)}) %collective-permute-start.16) | collective-permute-done | bytes 36896 | tf_op jit(solution)/shard_map/ppermute | solution.py:33
  71.8 0.0 collective-permute-done.15
  71.8 3.9 %triangle.1 = f32[128,128]{1,0:T(8,128)} custom-call(f32[72,128]{1,0:T(8,128)S(1)} %add_add_fusion.2.gram), custom_call_target="tpu_custom_call" | custom-call | tf_op jit(solution)/shard_map/triangle/pallas_call | solution.py:441
  (6 shorter events, 0.1 us)
Async XLA Ops:
  0.6 25.6 %copy-start = (f32[256,32]{0,1:T(8,128)S(1)}, f32[256,32]{0,1:T(8,128)}, u32[]{:S(2)}) copy-start(f32[256,32]{0,1:T(8,128)} %param.3) | copy-start | bytes 98308
  5.6 1.5 %collective-permute-start = (f32[136,128]{1,0:T(8,128)S(1)}, f32[136,128]{1,0:T(8,128)S(1)}, u32[]{:S(2)}, u32[]{:S(2)}) collective-permute-start(f32[136,128]{1,0:T(8,128)S(1)} %get-tuple-element.17), channel_id=1, source_target_pairs={{0,8},{1,9},{2,10},{3,11},{4,12},{5,13},{6,14},{7,15},{8,0},{9,1},... | collective-permute-start | bytes 208904 | tf_op jit(solution)/shard_map/ppermute | solution.py:33
  7.1 6.3 %collective-permute-start.3 = (f32[136,128]{1,0:T(8,128)S(1)}, f32[136,128]{1,0:T(8,128)S(1)}, u32[]{:S(2)}, u32[]{:S(2)}) collective-permute-start(f32[136,128]{1,0:T(8,128)S(1)} %add.42), channel_id=1, source_target_pairs={{0,17},{1,16},{2,19},{3,18},{4,21},{5,20},{6,23},{7,22},{8,25},{9,... | collective-permute-start | bytes 208904 | tf_op jit(solution)/shard_map/ppermute | solution.py:33
  11.0 4.3 %collective-permute-start.2 = (f32[136,128]{1,0:T(8,128)S(1)}, f32[136,128]{1,0:T(8,128)S(1)}, u32[]{:S(2)}, u32[]{:S(2)}) collective-permute-start(f32[136,128]{1,0:T(8,128)S(1)} %add.42), channel_id=1, source_target_pairs={{0,1},{1,0},{2,3},{3,2},{4,5},{5,4},{6,7},{7,6},{8,9},{9,8},{10,11... | collective-permute-start | bytes 208904 | tf_op jit(solution)/shard_map/ppermute | solution.py:33
  11.5 4.3 %collective-permute-start.1 = (f32[136,128]{1,0:T(8,128)S(1)}, f32[136,128]{1,0:T(8,128)S(1)}, u32[]{:S(2)}, u32[]{:S(2)}) collective-permute-start(f32[136,128]{1,0:T(8,128)S(1)} %add.42), channel_id=1, source_target_pairs={{0,16},{1,17},{2,18},{3,19},{4,20},{5,21},{6,22},{7,23},{8,24},{9,... | collective-permute-start | bytes 208904 | tf_op jit(solution)/shard_map/ppermute | solution.py:33
  15.8 6.3 %collective-permute-start.6 = (f32[136,128]{1,0:T(8,128)S(1)}, f32[136,128]{1,0:T(8,128)S(1)}, u32[]{:S(2)}, u32[]{:S(2)}) collective-permute-start(f32[136,128]{1,0:T(8,128)S(1)} %add_add_fusion.1), channel_id=1, source_target_pairs={{0,6},{1,7},{2,4},{3,5},{4,2},{5,3},{6,0},{7,1},{8,14},{9,15},{10,... | collective-permute-start | bytes 208904 | tf_op jit(solution)/shard_map/ppermute | solution.py:33
  19.5 5.5 %collective-permute-start.5 = (f32[136,128]{1,0:T(8,128)S(1)}, f32[136,128]{1,0:T(8,128)S(1)}, u32[]{:S(2)}, u32[]{:S(2)}) collective-permute-start(f32[136,128]{1,0:T(8,128)S(1)} %add_add_fusion.1), channel_id=1, source_target_pairs={{0,4},{1,5},{2,6},{3,7},{4,0},{5,1},{6,2},{7,3},{8,12},{9,13},{10,... | collective-permute-start | bytes 208904 | tf_op jit(solution)/shard_map/ppermute | solution.py:33
  19.5 5.5 %collective-permute-start.4 = (f32[136,128]{1,0:T(8,128)S(1)}, f32[136,128]{1,0:T(8,128)S(1)}, u32[]{:S(2)}, u32[]{:S(2)}) collective-permute-start(f32[136,128]{1,0:T(8,128)S(1)} %add_add_fusion.1), channel_id=1, source_target_pairs={{0,2},{1,3},{2,0},{3,1},{4,6},{5,7},{6,4},{7,5},{8,10},{9,11},{10,... | collective-permute-start | bytes 208904 | tf_op jit(solution)/shard_map/ppermute | solution.py:33
  24.9 1.3 %collective-permute-start.7 = (f32[136,128]{1,0:T(8,128)S(1)}, f32[136,128]{1,0:T(8,128)S(1)}, u32[]{:S(2)}, u32[]{:S(2)}) collective-permute-start(f32[136,128]{1,0:T(8,128)S(1)} %add_add_fusion.mine), channel_id=1, source_target_pairs={{0,8},{1,9},{2,10},{3,11},{4,12},{5,13},{6,14},{7,15},{8,0},{9,1},... | collective-permute-start | bytes 208904 | tf_op jit(solution)/shard_map/ppermute | solution.py:33
  40.9 1.9 %collective-permute-start.8 = (f32[4,32,512]{2,1,0:T(8,128)S(1)}, f32[4,32,512]{2,1,0:T(8,128)S(1)}, u32[]{:S(2)}, u32[]{:S(2)}) collective-permute-start(f32[4,32,512]{2,1,0:T(8,128)S(1)} %get-tuple-element.25), channel_id=1, source_target_pairs={{0,8},{1,9},{2,10},{3,11},{4,12},{5,13},{6,14},{7,15},{8,0},{9,1},... | collective-permute-start | bytes 786440 | tf_op jit(solution)/shard_map/ppermute | solution.py:33
  41.0 9.2 %collective-permute-start.9 = (f32[4,32,512]{2,1,0:T(8,128)S(1)}, f32[4,32,512]{2,1,0:T(8,128)S(1)}, u32[]{:S(2)}, u32[]{:S(2)}) collective-permute-start(f32[4,32,512]{2,1,0:T(8,128)S(1)} %shard_map.49), channel_id=1, source_target_pairs={{0,16},{1,17},{2,18},{3,19},{4,20},{5,21},{6,22},{7,23},{8,24},{9,... | collective-permute-start | bytes 786440 | tf_op jit(solution)/shard_map/ppermute | solution.py:33
  42.5 12.0 %collective-permute-start.10 = (f32[4,32,512]{2,1,0:T(8,128)S(1)}, f32[4,32,512]{2,1,0:T(8,128)S(1)}, u32[]{:S(2)}, u32[]{:S(2)}) collective-permute-start(f32[4,32,512]{2,1,0:T(8,128)S(1)} %shard_map.50), channel_id=1, source_target_pairs={{0,24},{1,25},{2,26},{3,27},{4,28},{5,29},{6,30},{7,31},{8,16},{9,... | collective-permute-start | bytes 786440 | tf_op jit(solution)/shard_map/ppermute | solution.py:33
  56.0 1.3 %collective-permute-start.11 = (f32[72,128]{1,0:T(8,128)S(1)}, f32[72,128]{1,0:T(8,128)S(1)}, u32[]{:S(2)}, u32[]{:S(2)}) collective-permute-start(f32[72,128]{1,0:T(8,128)S(1)} %product.1), channel_id=1, source_target_pairs={{0,8},{1,9},{2,10},{3,11},{4,12},{5,13},{6,14},{7,15},{8,0},{9,1},... | collective-permute-start | bytes 110600 | tf_op jit(solution)/shard_map/ppermute | solution.py:33
  57.3 4.9 %collective-permute-start.14 = (f32[72,128]{1,0:T(8,128)S(1)}, f32[72,128]{1,0:T(8,128)S(1)}, u32[]{:S(2)}, u32[]{:S(2)}) collective-permute-start(f32[72,128]{1,0:T(8,128)S(1)} %add.49), channel_id=1, source_target_pairs={{0,17},{1,16},{2,19},{3,18},{4,21},{5,20},{6,23},{7,22},{8,25},{9,... | collective-permute-start | bytes 110600 | tf_op jit(solution)/shard_map/ppermute | solution.py:33
  58.8 4.0 %collective-permute-start.13 = (f32[72,128]{1,0:T(8,128)S(1)}, f32[72,128]{1,0:T(8,128)S(1)}, u32[]{:S(2)}, u32[]{:S(2)}) collective-permute-start(f32[72,128]{1,0:T(8,128)S(1)} %add.49), channel_id=1, source_target_pairs={{0,1},{1,0},{2,3},{3,2},{4,5},{5,4},{6,7},{7,6},{8,9},{9,8},{10,11... | collective-permute-start | bytes 110600 | tf_op jit(solution)/shard_map/ppermute | solution.py:33
  60.3 4.0 %collective-permute-start.12 = (f32[72,128]{1,0:T(8,128)S(1)}, f32[72,128]{1,0:T(8,128)S(1)}, u32[]{:S(2)}, u32[]{:S(2)}) collective-permute-start(f32[72,128]{1,0:T(8,128)S(1)} %add.49), channel_id=1, source_target_pairs={{0,16},{1,17},{2,18},{3,19},{4,20},{5,21},{6,22},{7,23},{8,24},{9,... | collective-permute-start | bytes 110600 | tf_op jit(solution)/shard_map/ppermute | solution.py:33
  64.2 5.9 %collective-permute-start.17 = (f32[72,128]{1,0:T(8,128)S(1)}, f32[72,128]{1,0:T(8,128)S(1)}, u32[]{:S(2)}, u32[]{:S(2)}) collective-permute-start(f32[72,128]{1,0:T(8,128)S(1)} %add_add_fusion.3), channel_id=1, source_target_pairs={{0,6},{1,7},{2,4},{3,5},{4,2},{5,3},{6,0},{7,1},{8,14},{9,15},{10,... | collective-permute-start | bytes 110600 | tf_op jit(solution)/shard_map/ppermute | solution.py:33
  66.9 4.9 %collective-permute-start.16 = (f32[72,128]{1,0:T(8,128)S(1)}, f32[72,128]{1,0:T(8,128)S(1)}, u32[]{:S(2)}, u32[]{:S(2)}) collective-permute-start(f32[72,128]{1,0:T(8,128)S(1)} %add_add_fusion.3), channel_id=1, source_target_pairs={{0,4},{1,5},{2,6},{3,7},{4,0},{5,1},{6,2},{7,3},{8,12},{9,13},{10,... | collective-permute-start | bytes 110600 | tf_op jit(solution)/shard_map/ppermute | solution.py:33
  66.9 4.9 %collective-permute-start.15 = (f32[72,128]{1,0:T(8,128)S(1)}, f32[72,128]{1,0:T(8,128)S(1)}, u32[]{:S(2)}, u32[]{:S(2)}) collective-permute-start(f32[72,128]{1,0:T(8,128)S(1)} %add_add_fusion.3), channel_id=1, source_target_pairs={{0,2},{1,3},{2,0},{3,1},{4,6},{5,7},{6,4},{7,5},{8,10},{9,11},{10,... | collective-permute-start | bytes 110600 | tf_op jit(solution)/shard_map/ppermute | solution.py:33

commit v2 on v1

--- a/solution.py
+++ b/solution.py
@@ -458,15 +458,15 @@
     mine = summed(mine + partner(other, 1))
     other = partner(mine, 1)
     basis, image, gram = begin(place, mine, other, start_basis.T)
-    far = []
+    far = {}
     share = y_cells // x_parts
     for d, skip, count in far_pieces(x_parts, share):
         piece = contract_ahead(place, held, image, x_cells, y_cells, species, share, d, skip, count)
-        far.append(partner(piece, d))
+        far[d] = partner(piece, d)
     basis_rows, basis, factor = finish(basis, gram)
     core_tensor, *near = contract(place, held, basis, x_cells, y_cells, species, x_parts)
     near = [partner(piece, d) if d else piece for d, piece in enumerate(near)]
-    gram_x = product(place, factor, near, far)
+    gram_x = product(place, factor, near, [far[d] for d in sorted(far)])
     gram_x = summed(gram_x + partner(gram_x, 1))
     column_count = y_cells * lax.axis_size("gy") * species * rank_kept
     x_triangle = triangle(gram_x, 1.0 / column_count**0.5)
@@ -474,7 +474,7 @@
 
 
 def far_pieces(x_parts, share):
-    return [(d, 0, share) for d in range(x_parts // 2, x_parts)]
+    return [(d, 0, share) for d in reversed(range(x_parts // 2, x_parts))]
 
 
 def solution(mesh):

time: 75.9 us -> 75.9 us (level)
  no operation moved by 1% of the time
where the time goes in v2:
time: 75.9 us; the launch traced here: 75.8 us
  waiting for transfers between devices  30.3 us (40%)
  Pallas kernels  24.9 us (33%)
  starting transfers between devices  19.8 us (26%)
    ppermute x18, waiting for transfers between devices, partner(): return lax.ppermute(value, ('gx', 'gy'), pairs)  30.3 us
    ppermute x18, starting transfers between devices, partner(): return lax.ppermute(value, ('gx', 'gy'), pairs)  19.8 us
    pallas_call x1, Pallas kernels, local_gram(): pl.pallas_call(functools.partial(gram_kernel, cuts), out_shape=[out, out,...  4.99 us
    pallas_call x1, Pallas kernels, contract(): pl.pallas_call(functools.partial(core_kernel, species, y_cells), grid=(st...  4.43 us
    pallas_call x1, Pallas kernels, triangle(): pl.pallas_call(functools.partial(triangle_kernel, scale), out_shape=jax.S...  3.95 us
    pallas_call x1, Pallas kernels, finish(): pl.pallas_call(finish_kernel, out_shape=[jax.ShapeDtypeStruct((rank, z),...  3.52 us
    pallas_call x1, Pallas kernels, begin(): pl.pallas_call(begin_kernel, out_shape=[rows, rows, jax.ShapeDtypeStruct(...  3.5 us
    pallas_call x2, Pallas kernels, contract_ahead(): pl.pallas_call(functools.partial(ahead_kernel, d, share, skip, species),...  3.13 us
  transfers between devices with their start and end apart: 18, of which 15 were waited for; matrix products, arithmetic and copies ran while one was open for 0% of the time, Pallas kernels for 0%

profile of v2, /device:TPU:0, one launch (start us, length us, event | category | flops | bytes accessed | tf_op | source)
XLA Modules:
  0.0 75.8 jit_solution(16297188402200736809)
XLA Ops:
  0.6 0.0 copy-start
  0.6 5.0 %gram.1 = (f32[136,128]{1,0:T(8,128)S(1)}, f32[136,128]{1,0:T(8,128)S(1)}, f32[8192,256]{1,0:T(8,128)S(1)}) custom-call(s32[1]{0:T(128)} %bitcast.place, f32[8192,256]{1,0:T(8,128)} %bitcast.9), custom_call_target="tpu_custom_call" | custom-call | tf_op jit(solution)/shard_map/gram/pallas_call | solution.py:212
  5.6 0.6 collective-permute-start
  6.2 0.9 %collective-permute-done = f32[136,128]{1,0:T(8,128)S(1)} collective-permute-done((f32[136,128]{1,0:T(8,128)S(1)}, f32[136,128]{1,0:T(8,128)S(1)}, u32[]{:S(2)}, u32[]{:S(2)}) %collective-permute-start) | collective-permute-done | bytes 69664 | tf_op jit(solution)/shard_map/ppermute | solution.py:33
  7.1 3.8 %collective-permute-start.3 = (f32[136,128]{1,0:T(8,128)S(1)}, f32[136,128]{1,0:T(8,128)S(1)}, u32[]{:S(2)}, u32[]{:S(2)}) collective-permute-start(f32[136,128]{1,0:T(8,128)S(1)} %add.42), channel_id=1, source_target_pairs={{0,17},{1,16},{2,19},{3,18},{4,21},{5,20},{6,23},{7,22},{8,25},{9,... | collective-permute-start | bytes 208904 | tf_op jit(solution)/shard_map/ppermute | solution.py:33
  11.0 0.5 collective-permute-start.2
  11.5 0.1 collective-permute-start.1
  11.6 1.9 %collective-permute-done.3 = f32[136,128]{1,0:T(8,128)S(1)} collective-permute-done((f32[136,128]{1,0:T(8,128)S(1)}, f32[136,128]{1,0:T(8,128)S(1)}, u32[]{:S(2)}, u32[]{:S(2)}) %collective-permute-start.3) | collective-permute-done | bytes 69664 | tf_op jit(solution)/shard_map/ppermute | solution.py:33
  13.5 1.8 %collective-permute-done.2 = f32[136,128]{1,0:T(8,128)S(1)} collective-permute-done((f32[136,128]{1,0:T(8,128)S(1)}, f32[136,128]{1,0:T(8,128)S(1)}, u32[]{:S(2)}, u32[]{:S(2)}) %collective-permute-start.2) | collective-permute-done | bytes 69664 | tf_op jit(solution)/shard_map/ppermute | solution.py:33
  15.3 0.5 collective-permute-done.1
  15.8 3.7 %collective-permute-start.6 = (f32[136,128]{1,0:T(8,128)S(1)}, f32[136,128]{1,0:T(8,128)S(1)}, u32[]{:S(2)}, u32[]{:S(2)}) collective-permute-start(f32[136,128]{1,0:T(8,128)S(1)} %add_add_fusion.1), channel_id=1, source_target_pairs={{0,6},{1,7},{2,4},{3,5},{4,2},{5,3},{6,0},{7,1},{8,14},{9,15},{10,... | collective-permute-start | bytes 208904 | tf_op jit(solution)/shard_map/ppermute | solution.py:33
  19.5 0.0 collective-permute-start.5
  19.5 0.8 %collective-permute-start.4 = (f32[136,128]{1,0:T(8,128)S(1)}, f32[136,128]{1,0:T(8,128)S(1)}, u32[]{:S(2)}, u32[]{:S(2)}) collective-permute-start(f32[136,128]{1,0:T(8,128)S(1)} %add_add_fusion.1), channel_id=1, source_target_pairs={{0,2},{1,3},{2,0},{3,1},{4,6},{5,7},{6,4},{7,5},{8,10},{9,11},{10,... | collective-permute-start | bytes 208904 | tf_op jit(solution)/shard_map/ppermute | solution.py:33
  20.3 1.9 %collective-permute-done.6 = f32[136,128]{1,0:T(8,128)S(1)} collective-permute-done((f32[136,128]{1,0:T(8,128)S(1)}, f32[136,128]{1,0:T(8,128)S(1)}, u32[]{:S(2)}, u32[]{:S(2)}) %collective-permute-start.6) | collective-permute-done | bytes 69664 | tf_op jit(solution)/shard_map/ppermute | solution.py:33
  22.1 2.8 %collective-permute-done.5 = f32[136,128]{1,0:T(8,128)S(1)} collective-permute-done((f32[136,128]{1,0:T(8,128)S(1)}, f32[136,128]{1,0:T(8,128)S(1)}, u32[]{:S(2)}, u32[]{:S(2)}) %collective-permute-start.5) | collective-permute-done | bytes 69664 | tf_op jit(solution)/shard_map/ppermute | solution.py:33
  24.9 0.0 collective-permute-done.4
  24.9 0.1 collective-permute-start.7
  25.0 1.2 %collective-permute-done.7.other = f32[136,128]{1,0:T(8,128)S(1)} collective-permute-done((f32[136,128]{1,0:T(8,128)S(1)}, f32[136,128]{1,0:T(8,128)S(1)}, u32[]{:S(2)}, u32[]{:S(2)}) %collective-permute-start.7) | collective-permute-done | bytes 69664 | tf_op jit(solution)/shard_map/ppermute | solution.py:33
  26.3 0.0 copy-done
  26.3 3.5 %begin.1 = (f32[32,256]{1,0:T(8,128)S(1)}, f32[32,256]{1,0:T(8,128)S(1)}, f32[256,256]{1,0:T(8,128)S(1)}) custom-call(s32[1]{0:T(128)} %bitcast.place, f32[136,128]{1,0:T(8,128)S(1)} %add_add_fusion.mine, f32[136,128]{1,0:T(8,128)S(1)} %collective-permute-done.7.other, f32[32,256]{1,0:T(8,128)S(1)} %bitcast.8), custom_call_target="tpu_custom_call" | custom-call | tf_op jit(solution)/shard_map/begin/pallas_call | solution.py:250
  29.8 1.6 %shard_map.50 = f32[4,32,512]{2,1,0:T(8,128)S(1)} custom-call(s32[1]{0:T(128)} %bitcast.place, f32[32,256,256]{2,1,0:T(8,128)S(1)} %bitcast.6, f32[32,256]{1,0:T(8,128)S(1)} %get-tuple-element.26.image), custom_call_target="tpu_custom_call" | custom-call | flops 1073741824 | bytes 4194304 | tf_op jit(solution)/shard_map/pallas_call | solution.py:302
  31.3 1.6 %shard_map.49 = f32[4,32,512]{2,1,0:T(8,128)S(1)} custom-call(s32[1]{0:T(128)} %bitcast.place, f32[32,256,256]{2,1,0:T(8,128)S(1)} %bitcast.7, f32[32,256]{1,0:T(8,128)S(1)} %get-tuple-element.26.image), custom_call_target="tpu_custom_call" | custom-call | flops 1073741824 | bytes 4194304 | tf_op jit(solution)/shard_map/pallas_call | solution.py:302
  32.9 3.5 %finish.1 = (f32[32,256]{1,0:T(8,128)}, f32[32,256]{1,0:T(8,128)S(1)}, f32[32,32]{1,0:T(8,128)S(1)}) custom-call(f32[32,256]{1,0:T(8,128)S(1)} %get-tuple-element.18.basis, f32[256,256]{1,0:T(8,128)S(1)} %get-tuple-element.19.gram), custom_call_target="tpu_custom_call" | custom-call | flops 1073741824 | bytes 16777216 | tf_op jit(solution)/shard_map/finish/pallas_call | solution.py:274
  36.4 4.4 %core.1 = (f32[512,512]{1,0:T(8,128)}, f32[4,32,512]{2,1,0:T(8,128)S(1)}, f32[4,32,512]{2,1,0:T(8,128)S(1)}) custom-call(s32[1]{0:T(128)} %bitcast.place, f32[8192,256]{1,0:T(8,128)S(1)} %get-tuple-element.15.field, f32[32,256]{1,0:T(8,128)S(1)} %get-tuple-element.20.basis), custom_call_target="tpu_custom_call" | custom-call | flops 2147483648 | bytes 16777216 | tf_op jit(solution)/shard_map/core/pallas_call | solution.py:345
  40.9 0.2 collective-permute-start.8
  41.0 1.5 %collective-permute-start.9 = (f32[4,32,512]{2,1,0:T(8,128)S(1)}, f32[4,32,512]{2,1,0:T(8,128)S(1)}, u32[]{:S(2)}, u32[]{:S(2)}) collective-permute-start(f32[4,32,512]{2,1,0:T(8,128)S(1)} %shard_map.49), channel_id=1, source_target_pairs={{0,16},{1,17},{2,18},{3,19},{4,20},{5,21},{6,22},{7,23},{8,24},{9,... | collective-permute-start | bytes 786440 | tf_op jit(solution)/shard_map/ppermute | solution.py:33
  42.5 0.2 collective-permute-start.10
  42.7 0.0 collective-permute-done.8.refs_1_
  42.7 7.5 %collective-permute-done.9.refs_2_ = f32[4,32,512]{2,1,0:T(8,128)S(1)} collective-permute-done((f32[4,32,512]{2,1,0:T(8,128)S(1)}, f32[4,32,512]{2,1,0:T(8,128)S(1)}, u32[]{:S(2)}, u32[]{:S(2)}) %collective-permute-start.9) | collective-permute-done | bytes 262176 | tf_op jit(solution)/shard_map/ppermute | solution.py:33
  50.2 4.4 %collective-permute-done.10.refs_3_ = f32[4,32,512]{2,1,0:T(8,128)S(1)} collective-permute-done((f32[4,32,512]{2,1,0:T(8,128)S(1)}, f32[4,32,512]{2,1,0:T(8,128)S(1)}, u32[]{:S(2)}, u32[]{:S(2)}) %collective-permute-start.10) | collective-permute-done | bytes 262176 | tf_op jit(solution)/shard_map/ppermute | solution.py:33
  54.6 1.4 %product.1 = f32[72,128]{1,0:T(8,128)S(1)} custom-call(s32[1]{0:T(128)} %bitcast.place, f32[32,32]{1,0:T(8,128)S(1)} %get-tuple-element.23.factor, f32[4,32,512]{2,1,0:T(8,128)S(1)} %get-tuple-element.24.refs_0_, f32[4,32,512]{2,1,0:T(8,128)S(1)} %collective-permute-done.8.refs_1_, f32[4,32,512]{2,1,0:T(8,128)S(1)} %collective-permute-done.9.refs_2_, ...), custom_call_target="tpu_custom_call" | custom-call | tf_op jit(solution)/shard_map/product/pallas_call | solution.py:420
  56.0 0.4 collective-permute-start.11
  56.4 0.9 %collective-permute-done.11 = f32[72,128]{1,0:T(8,128)S(1)} collective-permute-done((f32[72,128]{1,0:T(8,128)S(1)}, f32[72,128]{1,0:T(8,128)S(1)}, u32[]{:S(2)}, u32[]{:S(2)}) %collective-permute-start.11) | collective-permute-done | bytes 36896 | tf_op jit(solution)/shard_map/ppermute | solution.py:33
  57.3 1.5 %collective-permute-start.14 = (f32[72,128]{1,0:T(8,128)S(1)}, f32[72,128]{1,0:T(8,128)S(1)}, u32[]{:S(2)}, u32[]{:S(2)}) collective-permute-start(f32[72,128]{1,0:T(8,128)S(1)} %add.49), channel_id=1, source_target_pairs={{0,17},{1,16},{2,19},{3,18},{4,21},{5,20},{6,23},{7,22},{8,25},{9,... | collective-permute-start | bytes 110600 | tf_op jit(solution)/shard_map/ppermute | solution.py:33
  58.8 1.5 %collective-permute-start.13 = (f32[72,128]{1,0:T(8,128)S(1)}, f32[72,128]{1,0:T(8,128)S(1)}, u32[]{:S(2)}, u32[]{:S(2)}) collective-permute-start(f32[72,128]{1,0:T(8,128)S(1)} %add.49), channel_id=1, source_target_pairs={{0,1},{1,0},{2,3},{3,2},{4,5},{5,4},{6,7},{7,6},{8,9},{9,8},{10,11... | collective-permute-start | bytes 110600 | tf_op jit(solution)/shard_map/ppermute | solution.py:33
  60.3 0.5 collective-permute-start.12
  60.8 1.4 %collective-permute-done.14 = f32[72,128]{1,0:T(8,128)S(1)} collective-permute-done((f32[72,128]{1,0:T(8,128)S(1)}, f32[72,128]{1,0:T(8,128)S(1)}, u32[]{:S(2)}, u32[]{:S(2)}) %collective-permute-start.14) | collective-permute-done | bytes 36896 | tf_op jit(solution)/shard_map/ppermute | solution.py:33
  62.1 0.6 collective-permute-done.13
  62.8 1.5 %collective-permute-done.12 = f32[72,128]{1,0:T(8,128)S(1)} collective-permute-done((f32[72,128]{1,0:T(8,128)S(1)}, f32[72,128]{1,0:T(8,128)S(1)}, u32[]{:S(2)}, u32[]{:S(2)}) %collective-permute-start.12) | collective-permute-done | bytes 36896 | tf_op jit(solution)/shard_map/ppermute | solution.py:33
  64.2 2.7 %collective-permute-start.17 = (f32[72,128]{1,0:T(8,128)S(1)}, f32[72,128]{1,0:T(8,128)S(1)}, u32[]{:S(2)}, u32[]{:S(2)}) collective-permute-start(f32[72,128]{1,0:T(8,128)S(1)} %add_add_fusion.3), channel_id=1, source_target_pairs={{0,6},{1,7},{2,4},{3,5},{4,2},{5,3},{6,0},{7,1},{8,14},{9,15},{10,... | collective-permute-start | bytes 110600 | tf_op jit(solution)/shard_map/ppermute | solution.py:33
  66.9 0.0 collective-permute-start.16
  66.9 1.7 %collective-permute-start.15 = (f32[72,128]{1,0:T(8,128)S(1)}, f32[72,128]{1,0:T(8,128)S(1)}, u32[]{:S(2)}, u32[]{:S(2)}) collective-permute-start(f32[72,128]{1,0:T(8,128)S(1)} %add_add_fusion.3), channel_id=1, source_target_pairs={{0,2},{1,3},{2,0},{3,1},{4,6},{5,7},{6,4},{7,5},{8,10},{9,11},{10,... | collective-permute-start | bytes 110600 | tf_op jit(solution)/shard_map/ppermute | solution.py:33
  68.7 1.4 %collective-permute-done.17 = f32[72,128]{1,0:T(8,128)S(1)} collective-permute-done((f32[72,128]{1,0:T(8,128)S(1)}, f32[72,128]{1,0:T(8,128)S(1)}, u32[]{:S(2)}, u32[]{:S(2)}) %collective-permute-start.17) | collective-permute-done | bytes 36896 | tf_op jit(solution)/shard_map/ppermute | solution.py:33
  70.1 1.7 %collective-permute-done.16 = f32[72,128]{1,0:T(8,128)S(1)} collective-permute-done((f32[72,128]{1,0:T(8,128)S(1)}, f32[72,128]{1,0:T(8,128)S(1)}, u32[]{:S(2)}, u32[]{:S(2)}) %collective-permute-start.16) | collective-permute-done | bytes 36896 | tf_op jit(solution)/shard_map/ppermute | solution.py:33
  71.8 0.0 collective-permute-done.15
  71.8 3.9 %triangle.1 = f32[128,128]{1,0:T(8,128)} custom-call(f32[72,128]{1,0:T(8,128)S(1)} %add_add_fusion.2.gram), custom_call_target="tpu_custom_call" | custom-call | tf_op jit(solution)/shard_map/triangle/pallas_call | solution.py:441
  (6 shorter events, 0.1 us)
Async XLA Ops:
  0.6 25.6 %copy-start = (f32[256,32]{0,1:T(8,128)S(1)}, f32[256,32]{0,1:T(8,128)}, u32[]{:S(2)}) copy-start(f32[256,32]{0,1:T(8,128)} %param.3) | copy-start | bytes 98308
  5.6 1.5 %collective-permute-start = (f32[136,128]{1,0:T(8,128)S(1)}, f32[136,128]{1,0:T(8,128)S(1)}, u32[]{:S(2)}, u32[]{:S(2)}) collective-permute-start(f32[136,128]{1,0:T(8,128)S(1)} %get-tuple-element.17), channel_id=1, source_target_pairs={{0,8},{1,9},{2,10},{3,11},{4,12},{5,13},{6,14},{7,15},{8,0},{9,1},... | collective-permute-start | bytes 208904 | tf_op jit(solution)/shard_map/ppermute | solution.py:33
  7.1 6.3 %collective-permute-start.3 = (f32[136,128]{1,0:T(8,128)S(1)}, f32[136,128]{1,0:T(8,128)S(1)}, u32[]{:S(2)}, u32[]{:S(2)}) collective-permute-start(f32[136,128]{1,0:T(8,128)S(1)} %add.42), channel_id=1, source_target_pairs={{0,17},{1,16},{2,19},{3,18},{4,21},{5,20},{6,23},{7,22},{8,25},{9,... | collective-permute-start | bytes 208904 | tf_op jit(solution)/shard_map/ppermute | solution.py:33
  11.0 4.3 %collective-permute-start.2 = (f32[136,128]{1,0:T(8,128)S(1)}, f32[136,128]{1,0:T(8,128)S(1)}, u32[]{:S(2)}, u32[]{:S(2)}) collective-permute-start(f32[136,128]{1,0:T(8,128)S(1)} %add.42), channel_id=1, source_target_pairs={{0,1},{1,0},{2,3},{3,2},{4,5},{5,4},{6,7},{7,6},{8,9},{9,8},{10,11... | collective-permute-start | bytes 208904 | tf_op jit(solution)/shard_map/ppermute | solution.py:33
  11.5 4.3 %collective-permute-start.1 = (f32[136,128]{1,0:T(8,128)S(1)}, f32[136,128]{1,0:T(8,128)S(1)}, u32[]{:S(2)}, u32[]{:S(2)}) collective-permute-start(f32[136,128]{1,0:T(8,128)S(1)} %add.42), channel_id=1, source_target_pairs={{0,16},{1,17},{2,18},{3,19},{4,20},{5,21},{6,22},{7,23},{8,24},{9,... | collective-permute-start | bytes 208904 | tf_op jit(solution)/shard_map/ppermute | solution.py:33
  15.8 6.3 %collective-permute-start.6 = (f32[136,128]{1,0:T(8,128)S(1)}, f32[136,128]{1,0:T(8,128)S(1)}, u32[]{:S(2)}, u32[]{:S(2)}) collective-permute-start(f32[136,128]{1,0:T(8,128)S(1)} %add_add_fusion.1), channel_id=1, source_target_pairs={{0,6},{1,7},{2,4},{3,5},{4,2},{5,3},{6,0},{7,1},{8,14},{9,15},{10,... | collective-permute-start | bytes 208904 | tf_op jit(solution)/shard_map/ppermute | solution.py:33
  19.5 5.5 %collective-permute-start.5 = (f32[136,128]{1,0:T(8,128)S(1)}, f32[136,128]{1,0:T(8,128)S(1)}, u32[]{:S(2)}, u32[]{:S(2)}) collective-permute-start(f32[136,128]{1,0:T(8,128)S(1)} %add_add_fusion.1), channel_id=1, source_target_pairs={{0,4},{1,5},{2,6},{3,7},{4,0},{5,1},{6,2},{7,3},{8,12},{9,13},{10,... | collective-permute-start | bytes 208904 | tf_op jit(solution)/shard_map/ppermute | solution.py:33
  19.5 5.5 %collective-permute-start.4 = (f32[136,128]{1,0:T(8,128)S(1)}, f32[136,128]{1,0:T(8,128)S(1)}, u32[]{:S(2)}, u32[]{:S(2)}) collective-permute-start(f32[136,128]{1,0:T(8,128)S(1)} %add_add_fusion.1), channel_id=1, source_target_pairs={{0,2},{1,3},{2,0},{3,1},{4,6},{5,7},{6,4},{7,5},{8,10},{9,11},{10,... | collective-permute-start | bytes 208904 | tf_op jit(solution)/shard_map/ppermute | solution.py:33
  24.9 1.3 %collective-permute-start.7 = (f32[136,128]{1,0:T(8,128)S(1)}, f32[136,128]{1,0:T(8,128)S(1)}, u32[]{:S(2)}, u32[]{:S(2)}) collective-permute-start(f32[136,128]{1,0:T(8,128)S(1)} %add_add_fusion.mine), channel_id=1, source_target_pairs={{0,8},{1,9},{2,10},{3,11},{4,12},{5,13},{6,14},{7,15},{8,0},{9,1},... | collective-permute-start | bytes 208904 | tf_op jit(solution)/shard_map/ppermute | solution.py:33
  40.9 1.9 %collective-permute-start.8 = (f32[4,32,512]{2,1,0:T(8,128)S(1)}, f32[4,32,512]{2,1,0:T(8,128)S(1)}, u32[]{:S(2)}, u32[]{:S(2)}) collective-permute-start(f32[4,32,512]{2,1,0:T(8,128)S(1)} %get-tuple-element.25), channel_id=1, source_target_pairs={{0,8},{1,9},{2,10},{3,11},{4,12},{5,13},{6,14},{7,15},{8,0},{9,1},... | collective-permute-start | bytes 786440 | tf_op jit(solution)/shard_map/ppermute | solution.py:33
  41.0 9.2 %collective-permute-start.9 = (f32[4,32,512]{2,1,0:T(8,128)S(1)}, f32[4,32,512]{2,1,0:T(8,128)S(1)}, u32[]{:S(2)}, u32[]{:S(2)}) collective-permute-start(f32[4,32,512]{2,1,0:T(8,128)S(1)} %shard_map.49), channel_id=1, source_target_pairs={{0,16},{1,17},{2,18},{3,19},{4,20},{5,21},{6,22},{7,23},{8,24},{9,... | collective-permute-start | bytes 786440 | tf_op jit(solution)/shard_map/ppermute | solution.py:33
  42.5 12.0 %collective-permute-start.10 = (f32[4,32,512]{2,1,0:T(8,128)S(1)}, f32[4,32,512]{2,1,0:T(8,128)S(1)}, u32[]{:S(2)}, u32[]{:S(2)}) collective-permute-start(f32[4,32,512]{2,1,0:T(8,128)S(1)} %shard_map.50), channel_id=1, source_target_pairs={{0,24},{1,25},{2,26},{3,27},{4,28},{5,29},{6,30},{7,31},{8,16},{9,... | collective-permute-start | bytes 786440 | tf_op jit(solution)/shard_map/ppermute | solution.py:33
  56.0 1.3 %collective-permute-start.11 = (f32[72,128]{1,0:T(8,128)S(1)}, f32[72,128]{1,0:T(8,128)S(1)}, u32[]{:S(2)}, u32[]{:S(2)}) collective-permute-start(f32[72,128]{1,0:T(8,128)S(1)} %product.1), channel_id=1, source_target_pairs={{0,8},{1,9},{2,10},{3,11},{4,12},{5,13},{6,14},{7,15},{8,0},{9,1},... | collective-permute-start | bytes 110600 | tf_op jit(solution)/shard_map/ppermute | solution.py:33
  57.3 4.9 %collective-permute-start.14 = (f32[72,128]{1,0:T(8,128)S(1)}, f32[72,128]{1,0:T(8,128)S(1)}, u32[]{:S(2)}, u32[]{:S(2)}) collective-permute-start(f32[72,128]{1,0:T(8,128)S(1)} %add.49), channel_id=1, source_target_pairs={{0,17},{1,16},{2,19},{3,18},{4,21},{5,20},{6,23},{7,22},{8,25},{9,... | collective-permute-start | bytes 110600 | tf_op jit(solution)/shard_map/ppermute | solution.py:33
  58.8 4.0 %collective-permute-start.13 = (f32[72,128]{1,0:T(8,128)S(1)}, f32[72,128]{1,0:T(8,128)S(1)}, u32[]{:S(2)}, u32[]{:S(2)}) collective-permute-start(f32[72,128]{1,0:T(8,128)S(1)} %add.49), channel_id=1, source_target_pairs={{0,1},{1,0},{2,3},{3,2},{4,5},{5,4},{6,7},{7,6},{8,9},{9,8},{10,11... | collective-permute-start | bytes 110600 | tf_op jit(solution)/shard_map/ppermute | solution.py:33
  60.3 4.0 %collective-permute-start.12 = (f32[72,128]{1,0:T(8,128)S(1)}, f32[72,128]{1,0:T(8,128)S(1)}, u32[]{:S(2)}, u32[]{:S(2)}) collective-permute-start(f32[72,128]{1,0:T(8,128)S(1)} %add.49), channel_id=1, source_target_pairs={{0,16},{1,17},{2,18},{3,19},{4,20},{5,21},{6,22},{7,23},{8,24},{9,... | collective-permute-start | bytes 110600 | tf_op jit(solution)/shard_map/ppermute | solution.py:33
  64.2 5.9 %collective-permute-start.17 = (f32[72,128]{1,0:T(8,128)S(1)}, f32[72,128]{1,0:T(8,128)S(1)}, u32[]{:S(2)}, u32[]{:S(2)}) collective-permute-start(f32[72,128]{1,0:T(8,128)S(1)} %add_add_fusion.3), channel_id=1, source_target_pairs={{0,6},{1,7},{2,4},{3,5},{4,2},{5,3},{6,0},{7,1},{8,14},{9,15},{10,... | collective-permute-start | bytes 110600 | tf_op jit(solution)/shard_map/ppermute | solution.py:33
  66.9 4.9 %collective-permute-start.16 = (f32[72,128]{1,0:T(8,128)S(1)}, f32[72,128]{1,0:T(8,128)S(1)}, u32[]{:S(2)}, u32[]{:S(2)}) collective-permute-start(f32[72,128]{1,0:T(8,128)S(1)} %add_add_fusion.3), channel_id=1, source_target_pairs={{0,4},{1,5},{2,6},{3,7},{4,0},{5,1},{6,2},{7,3},{8,12},{9,13},{10,... | collective-permute-start | bytes 110600 | tf_op jit(solution)/shard_map/ppermute | solution.py:33
  66.9 4.9 %collective-permute-start.15 = (f32[72,128]{1,0:T(8,128)S(1)}, f32[72,128]{1,0:T(8,128)S(1)}, u32[]{:S(2)}, u32[]{:S(2)}) collective-permute-start(f32[72,128]{1,0:T(8,128)S(1)} %add_add_fusion.3), channel_id=1, source_target_pairs={{0,2},{1,3},{2,0},{3,1},{4,6},{5,7},{6,4},{7,5},{8,10},{9,11},{10,... | collective-permute-start | bytes 110600 | tf_op jit(solution)/shard_map/ppermute | solution.py:33
